TPU v7x, 512 devices: a whole 4x4x16 slice. The times are simulated.
512 devices in a mesh: dom: 64 (over y, z), mode: 8 (over x, core).
Axes of the slice: x: 4, y: 4, z: 16, core: 2. Of those that a mesh axis runs over, the one named last changes fastest.
Arguments:
- mode_basis: bfloat16 [3, 512, 65536], P(None, 'mode', 'dom'), may hold values from -6 to 6
- blocks: bfloat16 [16, 3, 3, 65536], P(None, None, None, 'dom'), may hold values from -0.875 to 0.875
- columns: int32 [16, 65536], P(None, 'dom'), may hold values from -256 to 257, as said below
- samples: int32 [512], replicated, may hold values from 0 to 196607, as said below
- inverse: bfloat16 [512, 512], replicated, may hold values from -0.25 to 0.25
Outputs:
- reduced: float32 [512, 512], P('dom', 'mode')
- coefficients: float32 [512, 512], P('dom', 'mode')
Inputs may be any that keep to these rules, and one draw needn't show every extreme that they name: `columns`: each entry is 256 + 1 (an empty slot) or an offset that keeps n + offset within 0 to 65535; slot 0 of every row holds offset 0. `samples`: 512 distinct dofs; half of them lie in the first half of the dofs.
All inputs are finite; a program needn't handle non-finite values.
Results may differ from a plain program's by a relative error of at most 0.0029.
Values may be sent and summed in bfloat16 or wider, within the bound.
No kernel may reach another device: no remote copies, remote signals or barrier semaphores. Data moves between devices by JAX's collectives and lax.ppermute only.
A program may use at most 64 MiB of HBM per device.

v0:
```python
import math

import jax
import jax.numpy as jnp
from jax import lax
from jax.sharding import PartitionSpec as P


def extended_2(x, sides, width):
    for axis, dim in sides:
        devices, length = (lax.axis_size(axis), x.shape[dim])
        up = [(i, (i + 1) % devices) for i in range(devices - 1)]
        down = [(j, i) for i, j in up]
        last = lax.slice_in_dim(x, length - width, length, axis=dim)
        initial = lax.slice_in_dim(x, 0, width, axis=dim)
        before = lax.ppermute(last, axis, up)
        after = lax.ppermute(initial, axis, down)
        x = jnp.concatenate([before, x, after], axis=dim)
    return x


def slot_products(extended, blocks, columns, halo_width, out_shape):
    local_ids = lax.broadcasted_iota(jnp.int32, (out_shape[2],), 0)

    def slot_step(slot_index, running):
        offset = columns[slot_index]
        usable = offset != halo_width + 1
        position = jnp.where(usable, local_ids + offset + halo_width, 0)
        nearby = jnp.take(extended, position, axis=2)
        weights = jnp.where(
            usable[None, None, :], blocks[slot_index].astype(jnp.float32), jnp.float32(0.0)
        )
        running = running + weights[:, 0, None, :] * nearby[0][None]
        running = running + weights[:, 1, None, :] * nearby[1][None]
        running = running + weights[:, 2, None, :] * nearby[2][None]
        return running

    return lax.fori_loop(0, blocks.shape[0], slot_step, jnp.zeros(out_shape, jnp.float32))


def shards(mode_basis, blocks, columns, samples, inverse):
    node_count = mode_basis.shape[2]
    halo_width = node_count // 4
    first_node = lax.axis_index("dom") * node_count
    extended = extended_2(mode_basis, (("dom", 2),), halo_width)
    image = slot_products(extended, blocks, columns, halo_width, mode_basis.shape).astype(
        jnp.bfloat16
    )
    scaling = 1.0 / math.sqrt(3 * node_count * lax.axis_size("dom"))
    reduced_part = jnp.einsum(
        "crn,csn->rs",
        lax.all_gather(mode_basis, "mode", axis=1, tiled=True),
        image,
        preferred_element_type=jnp.float32,
    )
    component = samples % 3
    node_index = samples // 3 - first_node
    owned_here = (node_index >= 0) & (node_index < node_count)
    node_local = jnp.where(owned_here, node_index, 0)
    chosen = image[component, :, node_local]
    chosen = jnp.where(owned_here[:, None], chosen, jnp.zeros_like(chosen))
    reduced = lax.psum_scatter(reduced_part, "dom", scatter_dimension=0, tiled=True)
    picked = lax.psum(chosen.astype(jnp.float32), "dom").astype(jnp.bfloat16)
    row_count = inverse.shape[0] // lax.axis_size("dom")
    inverse_rows = lax.dynamic_slice_in_dim(
        inverse, lax.axis_index("dom") * row_count, row_count, 0
    )
    coefficients = jnp.dot(inverse_rows, picked, preferred_element_type=jnp.float32)
    return (reduced * scaling, coefficients)


def solution(mesh):
    return jax.shard_map(
        shards,
        mesh=mesh,
        in_specs=(P(None, "mode", "dom"), P(None, None, None, "dom"), P(None, "dom"), P(), P()),
        out_specs=(P("dom", "mode"), P("dom", "mode")),
        check_vma=False,
    )
```

profile of v0, /device:TPU:2, one launch (start us, length us, event | category | flops | bytes accessed | tf_op | source)
XLA Modules:
  0.0 767.6 jit_solution(10623633482755351531)
XLA Ops:
  8.0 1.0 fusion.18
  8.9 1.3 collective-permute-start.1
  10.2 4.6 collective-permute-start
  15.5 1.2 copy.32
  16.8 1.3 dynamic-slice
  18.8 2.2 copy.33
  21.0 190.9 %while.15 = (s32[]{:T(128)}, f32[3,64,1024]{2,1,0:T(8,128)S(1)}, s32[16,1024]{1,0:T(8,128)}, bf16[16,3,3,1024]{3,1,2,0:T(4,128)(2,1)S(1)}, bf16[3,64,1536]{1,0,2:T(4,128)(2,1)}, /*index=5*/s32[]{:T(128)}, s32[]{:T(128)}) while((s32[]{:T(128)}, f32[3,64,1024]{2,1,0:T(8,128)S(1)}, s32[16,1024]{1,0:T(8,128)}, ...), condition=%wide.region_1.2_spmd.clone.clone, body=%wide.region_0.1_spmd.clone.clone.sunk | while | flops 1806339 | bytes 6883431 | solution.py:38
  21.8 5.0 gather_fusion
  26.7 3.8 select_bitcast_fusion.2
  30.5 1.1 slice_convert_fusion.4
  32.9 0.8 compare_select_fusion.6
  33.7 5.0 gather_fusion
  38.7 3.8 select_bitcast_fusion.2
  42.4 1.1 slice_convert_fusion.4
  44.8 0.8 compare_select_fusion.6
  45.6 5.0 gather_fusion
  50.6 3.8 select_bitcast_fusion.2
  54.4 1.1 slice_convert_fusion.4
  56.8 0.8 compare_select_fusion.6
  57.6 5.0 gather_fusion
  62.6 3.8 select_bitcast_fusion.2
  66.3 1.1 slice_convert_fusion.4
  69.5 5.0 gather_fusion
  74.5 3.8 select_bitcast_fusion.2
  78.3 1.1 slice_convert_fusion.4
  81.5 5.0 gather_fusion
  86.4 3.8 select_bitcast_fusion.2
  90.2 1.1 slice_convert_fusion.4
  93.4 5.0 gather_fusion
  98.4 3.8 select_bitcast_fusion.2
  102.1 1.1 slice_convert_fusion.4
  105.3 5.0 gather_fusion
  110.3 3.8 select_bitcast_fusion.2
  114.1 1.1 slice_convert_fusion.4
  117.3 5.0 gather_fusion
  122.2 3.8 select_bitcast_fusion.2
  126.0 1.1 slice_convert_fusion.4
  129.2 5.0 gather_fusion
  134.2 3.8 select_bitcast_fusion.2
  137.9 1.1 slice_convert_fusion.4
  141.1 5.0 gather_fusion
  146.1 3.8 select_bitcast_fusion.2
  149.9 1.1 slice_convert_fusion.4
  153.1 5.0 gather_fusion
  158.0 3.8 select_bitcast_fusion.2
  161.8 1.1 slice_convert_fusion.4
  165.0 5.0 gather_fusion
  170.0 3.8 select_bitcast_fusion.2
  173.7 1.1 slice_convert_fusion.4
  176.1 0.8 compare_select_fusion.6
  176.9 5.0 gather_fusion
  181.9 3.8 select_bitcast_fusion.2
  185.6 1.1 slice_convert_fusion.4
  188.8 5.0 gather_fusion
  193.8 3.8 select_bitcast_fusion.2
  197.6 1.1 slice_convert_fusion.4
  200.8 5.0 gather_fusion
  205.7 3.8 select_bitcast_fusion.2
  209.5 1.1 slice_convert_fusion.4
  212.3 3.2 gather_fusion.1
  215.7 285.6 %all-reduce.5 = bf16[512,64]{1,0:T(8,128)(2,1)S(1)} all-reduce(f32[512,64]{1,0:T(8,128)S(1)} %select_convert_fusion), channel_id=1, replica_groups=mesh['dom'=64,'mode'=8] {'dom'}, use_global_device_ids=true, to_apply=%region_3.4 | all-reduce | flops 32768 | bytes 196608 | tf_op jit(solution)/shard_map/psum | solution.py:63
  501.3 3.6 convolution_bitcast_fusion
  505.7 253.6 %all-reduce.4.cloned.1.call-done = f32[512,64]{0,1:T(8,128)} async-done(((f32[512,64]{0,1:T(8,128)}), f32[512,64]{0,1:T(8,128)}) %all-reduce.4.cloned.1.call-update) | async-done | bytes 131088
  759.3 0.8 dynamic-slice_multiply_fusion
  (159 shorter events, 33.1 us)
Async XLA Ops:
  7.2 497.8 %copy-start = (bf16[512,512]{1,0:T(8,128)(2,1)S(1)}, bf16[512,512]{1,0:T(8,128)(2,1)}, u32[]{:S(2)}) copy-start(bf16[512,512]{1,0:T(8,128)(2,1)} %param.11) | copy-start | bytes 1572868
  7.2 11.5 %copy-start.1 = (bf16[3,64,1024]{2,1,0:T(8,128)(2,1)S(1)}, bf16[3,64,1024]{2,1,0:T(8,128)(2,1)}, u32[]{:S(2)}) copy-start(bf16[3,64,1024]{2,1,0:T(8,128)(2,1)} %param.7) | copy-start | bytes 1179652
  7.2 494.1 %all-gather.2.cloned.1.call-start = ((), (), s32[]{:S(2)}) async-start(), calls=%async_computation | async-start | bytes 3538944 | tf_op jit(solution)/shard_map/all_gather | solution.py:52
  7.9 751.3 %all-reduce.4.cloned.1.call-start = ((), (), s32[]{:S(2)}) async-start(), calls=%async_computation.1 | async-start | bytes 262144
  8.9 9.7 %collective-permute-start.1 = (bf16[3,64,256]{2,1,0:T(8,128)(2,1)S(1)}, bf16[3,64,256]{2,1,0:T(8,128)(2,1)S(1)}, u32[]{:S(2)}, u32[]{:S(2)}) collective-permute-start(bf16[3,64,256]{2,1,0:T(8,128)(2,1)S(1)} %get-tuple-element.202), channel_id=1, source_target_pairs={{8,0},{16,8},{24,16},{32,24},{40,32},{48,40},{56,48},{64,56},{72,6... | collective-permute-start | bytes 294920 | tf_op jit(solution)/shard_map/ppermute | solution.py:17
  10.2 8.5 %collective-permute-start = (bf16[3,64,256]{2,1,0:T(8,128)(2,1)S(1)}, bf16[3,64,256]{2,1,0:T(8,128)(2,1)S(1)}, u32[]{:S(2)}, u32[]{:S(2)}) collective-permute-start(bf16[3,64,256]{2,1,0:T(8,128)(2,1)S(1)} %get-tuple-element.201), channel_id=1, source_target_pairs={{0,8},{8,16},{16,24},{24,32},{32,40},{40,48},{48,56},{56,64},{64,7... | collective-permute-start | bytes 294920 | tf_op jit(solution)/shard_map/ppermute | solution.py:16
Sparse Core Ops, SparseCore 0:
  10.1 38.8 all-gather.1
  505.0 254.1 all-reduce.3
where the time goes:
time: 769 us; the launch traced here: 768 us
  blocking collectives  286 us (37%)
  waiting for transfers between devices  254 us (33%)
  other arithmetic  103 us (13%)
  local copies, waits for them, and re-layouts  98 us (13%)
  between operations  14.8 us (2%)
    psum x1, blocking collectives, shards(): picked = lax.psum(chosen.astype(jnp.float32), 'dom').astype(jnp.bfloat16)  286 us
    unnamed x3, waiting for transfers between devices  254 us
    gather x16, local copies, waits for them, and re-layouts, slot_step(): nearby = jnp.take(extended, position, axis=2)  79.3 us
    select_n x32, other arithmetic, slot_step(): nearby = jnp.take(extended, position, axis=2)  72.5 us
    mul x16, other arithmetic, slot_step(): running = running + weights[:, 0, None, :] * nearby[0][None]  17.3 us
  transfers between devices with their start and end apart: 4, of which 1 were waited for; matrix products, arithmetic and copies ran while one was open for 26% of the time, Pallas kernels for 0%

commit v1 on v0

v1 whole, which is shorter than its diff:
```python
import functools
import math

import jax
import jax.numpy as jnp
from jax import lax
from jax.experimental import pallas as pl
from jax.experimental.pallas import tpu as pltpu
from jax.sharding import Mesh, PartitionSpec as P

DOM = ("y", "z")
MODE = ("x", "core")
F32 = jnp.float32
BF16 = jnp.bfloat16
LANES = 128


def stencil_kernel(columns_ref, weights_ref, before_ref, basis_ref, after_ref, image_ref, extended_ref, target_ref):
    slots, nodes = columns_ref.shape
    parts, modes, halo = before_ref.shape
    window = LANES + 2 * halo
    chunks = window // LANES
    for b in range(parts):
        rows = slice(b * modes, (b + 1) * modes)
        extended_ref[rows, 0:halo] = before_ref[b]
        extended_ref[rows, halo : halo + nodes] = basis_ref[b]
        extended_ref[rows, halo + nodes :] = after_ref[b]
    lane = lax.broadcasted_iota(jnp.int32, (slots, LANES), 1)
    row_ids = lax.broadcasted_iota(jnp.int32, (16, LANES), 0)
    one = jnp.ones((16, LANES), BF16)
    zero = jnp.zeros((16, LANES), BF16)
    ids = [(row_ids + 16 * q).astype(F32).astype(BF16) for q in range(LANES // 16)]

    def node_block(step, carry):
        first = pl.multiple_of(step * LANES, LANES)
        here = pl.ds(first, LANES)
        offset = columns_ref[:, here]
        target = jnp.where(offset == halo + 1, -window, lane + offset + halo)
        for k in range(chunks):
            target_ref[k * slots : (k + 1) * slots, :] = jnp.clip(target - LANES * k, -1, LANES).astype(F32)
        values = extended_ref[:, pl.ds(first, window)]
        sums = [jnp.zeros((modes, LANES), F32) for _ in range(parts)]
        for pair in range(slots // 2):
            both = []
            for j in (2 * pair, 2 * pair + 1):
                hits = []
                for k in range(chunks):
                    row = k * slots + j
                    wanted = jnp.broadcast_to(target_ref[row : row + 1, :], (16, LANES)).astype(BF16)
                    hits += [jnp.where(i == wanted, one, zero) for i in ids]
                both.append(jnp.concatenate(hits, axis=0))
            picked = jnp.dot(values, jnp.concatenate(both, axis=1), preferred_element_type=F32)
            for side in range(2):
                j = 2 * pair + side
                for b in range(parts):
                    nearby = picked[b * modes : (b + 1) * modes, side * LANES : (side + 1) * LANES]
                    for a in range(parts):
                        row = (j * parts + a) * parts + b
                        sums[a] = sums[a] + weights_ref[row : row + 1, here] * nearby
        for a in range(parts):
            image_ref[a, :, here] = sums[a].astype(BF16)
        return carry

    lax.fori_loop(0, nodes // LANES, node_block, 0)


def stencil(columns, weights, before, basis, after):
    slots, nodes = columns.shape
    parts, modes, halo = before.shape
    return pl.pallas_call(
        stencil_kernel,
        out_shape=jax.ShapeDtypeStruct(basis.shape, BF16),
        scratch_shapes=[
            pltpu.VMEM((parts * modes, nodes + 2 * halo), BF16),
            pltpu.VMEM((slots * (LANES + 2 * halo) // LANES, LANES), F32),
        ],
        name="stencil",
    )(columns, weights, before, basis, after)


def sampled_kernel(place_ref, inverse_ref, image_ref, out_ref):
    parts, modes, nodes = image_ref.shape
    samples = place_ref.shape[1]
    total = jnp.zeros((modes, samples), F32)
    for c in range(parts):
        for first in range(0, nodes, 256):
            ids = lax.broadcasted_iota(jnp.int32, (256, samples), 0) + (c * nodes + first)
            hit = jnp.where(ids == place_ref[...], 1.0, 0.0).astype(BF16)
            total = total + jnp.dot(image_ref[c, :, first : first + 256], hit, preferred_element_type=F32)
    out_ref[...] = lax.dot_general(
        inverse_ref[...], total.astype(BF16), (((1,), (1,)), ((), ())), preferred_element_type=F32
    )


def sampled(place, inverse, image):
    return pl.pallas_call(
        sampled_kernel,
        out_shape=jax.ShapeDtypeStruct((inverse.shape[0], image.shape[1]), F32),
        name="sampled",
    )(place, inverse, image)


def reduced_kernel(core_ref, mine_ref, theirs_ref, image_ref, sampled_ref, out_ref):
    chips, parts, modes, _ = mine_ref.shape
    core = core_ref[0]
    for x in range(chips):
        for source, ref in ((core, mine_ref), (1 - core, theirs_ref)):
            total = jnp.zeros((modes, modes), F32)
            for c in range(parts):
                total = total + lax.dot_general(
                    ref[x, c], image_ref[c], (((1,), (1,)), ((), ())), preferred_element_type=F32
                )
            first = pl.multiple_of((2 * x + source) * modes, modes)
            out_ref[pl.ds(first, modes), 0:modes] = total
    out_ref[:, modes : 2 * modes] = sampled_ref[...]


def reduced_rows(core, mine, theirs, image, sampled_part):
    chips, _, modes, _ = mine.shape
    return pl.pallas_call(
        reduced_kernel,
        in_specs=[pl.BlockSpec(memory_space=pltpu.SMEM)] + [pl.BlockSpec(memory_space=pltpu.VMEM)] * 4,
        out_specs=pl.BlockSpec(memory_space=pltpu.VMEM),
        out_shape=jax.ShapeDtypeStruct((2 * chips * modes, 2 * modes), F32),
        name="reduced",
    )(core, mine, theirs, image, sampled_part)


def shards(mode_basis, blocks, columns, samples, inverse):
    parts, modes, node_count = mode_basis.shape
    halo = node_count // 4
    chips = lax.axis_size("x")
    doms = lax.axis_size(DOM)
    dom = lax.axis_index(DOM)
    up = [(i, i + 1) for i in range(doms - 1)]
    down = [(i + 1, i) for i in range(doms - 1)]
    before = lax.ppermute(mode_basis[:, :, node_count - halo :], DOM, up)
    after = lax.ppermute(mode_basis[:, :, :halo], DOM, down)
    mine = lax.all_to_all(jnp.broadcast_to(mode_basis[None], (chips, *mode_basis.shape)), "x", 0, 0)
    weights = blocks.astype(F32).reshape(-1, node_count)
    image = stencil(columns, weights, before, mode_basis, after)
    node = samples // 3 - dom * node_count
    owned = (node >= 0) & (node < node_count)
    place = jnp.where(owned, (samples % 3) * node_count + node, -1)[None]
    sampled_part = sampled(place, inverse, image)
    theirs = lax.ppermute(mine, "core", [(0, 1), (1, 0)])
    core = lax.axis_index("core").astype(jnp.int32)[None]
    partial = reduced_rows(core, mine, theirs, image, sampled_part)
    pieces = lax.all_to_all(partial.reshape(doms, -1, 2 * modes), DOM, 0, 0)
    total = jnp.sum(pieces, axis=0)
    scaling = 1.0 / math.sqrt(3 * node_count * doms)
    return total[:, :modes] * scaling, total[:, modes:]


def solution(mesh):
    mesh = Mesh(mesh.devices.reshape(4, 16, 4, 2), DOM + MODE)
    return jax.shard_map(
        shards,
        mesh=mesh,
        in_specs=(P(None, MODE, DOM), P(None, None, None, DOM), P(None, DOM), P(), P()),
        out_specs=(P(DOM, MODE), P(DOM, MODE)),
        check_vma=False,
    )
```

time: 769 us -> 96 us (0.12)
  the two profiles are of different devices: /device:TPU:2 before, /device:TPU:8 now
where the time goes in v1:
time: 96 us; the launch traced here: 95.7 us
  blocking collectives  54.2 us (56%)
  Pallas kernels  16 us (17%)
  starting transfers between devices  15.1 us (16%)
  waiting for transfers between devices  4.99 us (5%)
  local copies, waits for them, and re-layouts  3.24 us (3%)
  other arithmetic  1.33 us (1%)
    all_to_all x1, blocking collectives, shards(): pieces = lax.all_to_all(partial.reshape(doms, -1, 2 * modes), DOM, 0, 0)  29.3 us
    all_to_all x1, blocking collectives, shards(): lax.all_to_all(jnp.broadcast_to(mode_basis[None], (chips, *mode_basis.sha...  24.9 us
    ppermute x1, starting transfers between devices, shards(): after = lax.ppermute(mode_basis[:, :, :halo], DOM, down)  11.3 us
    pallas_call x1, Pallas kernels, stencil(): pl.pallas_call(stencil_kernel, out_shape=jax.ShapeDtypeStruct(basis.shape...  9.47 us
    ppermute x1, waiting for transfers between devices, shards(): before = lax.ppermute(mode_basis[:, :, node_count - halo:], DOM, up)  4.98 us
    pallas_call x1, Pallas kernels, reduced_rows(): pl.pallas_call(reduced_kernel, in_specs=[pl.BlockSpec(memory_space=pltpu....  3.72 us
    pallas_call x1, Pallas kernels, sampled(): pl.pallas_call(sampled_kernel, out_shape=jax.ShapeDtypeStruct((inverse.sh...  2.81 us
    ppermute x1, starting transfers between devices, shards(): before = lax.ppermute(mode_basis[:, :, node_count - halo:], DOM, up)  1.92 us
  transfers between devices with their start and end apart: 3, of which 1 were waited for; matrix products, arithmetic and copies ran while one was open for 2% of the time, Pallas kernels for 13%

profile of v1, /device:TPU:8, one launch (start us, length us, event | category | flops | bytes accessed | tf_op | source)
XLA Modules:
  0.0 95.7 jit_solution(13547158585334293724)
XLA Ops:
  0.6 1.2 %broadcast_in_dim.15 = bf16[4,3,64,1024]{3,2,1,0:T(8,128)(2,1)S(1)} broadcast(bf16[3,64,1024]{2,1,0:T(8,128)(2,1)} %basis_ref.1), dimensions={1,2,3} | broadcast | bytes 1966080 | tf_op jit(solution)/shard_map/broadcast_in_dim | solution.py:139
  1.8 0.0 copy-start.1
  1.8 0.0 copy-start.5
  1.8 0.0 copy-start.2
  1.9 24.9 %all_to_all.10.mine_ref = bf16[4,3,64,1024]{3,2,1,0:T(8,128)(2,1)S(1)} all-to-all(bf16[4,3,64,1024]{3,2,1,0:T(8,128)(2,1)S(1)} %broadcast_in_dim.15), channel_id=1, replica_groups=mesh['y'=4,'z'=16,'x'=4,'core'=2] {'x'}, dimensions={0} | all-to-all | bytes 3145728 | tf_op jit(solution)/shard_map/all_to_all | solution.py:139
  26.8 0.0 copy-start
  26.8 1.9 %collective-permute-start = (bf16[4,3,64,1024]{3,2,1,0:T(8,128)(2,1)S(1)}, bf16[4,3,64,1024]{3,2,1,0:T(8,128)(2,1)}, u32[]{:S(2)}, u32[]{:S(2)}) collective-permute-start(bf16[4,3,64,1024]{3,2,1,0:T(8,128)(2,1)S(1)} %all_to_all.10.mine_ref), channel_id=1, source_target_pairs={{0,1},{1,0},{2,3},{3,2},{4,5},{5,4},{6,7},{7,6},{8,9},{9,8},{10,11... | collective-permute-start | bytes 4718600 | tf_op jit(solution)/shard_map/ppermute | solution.py:146
  28.7 0.0 copy-done.1
  28.7 11.3 %collective-permute-start.2 = (bf16[3,64,256]{2,1,0:T(8,128)(2,1)S(1)}, bf16[3,64,256]{2,1,0:T(8,128)(2,1)S(1)}, u32[]{:S(2)}, u32[]{:S(2)}) collective-permute-start(bf16[3,64,256]{2,1,0:T(8,128)(2,1)S(1)} %get-tuple-element.2), channel_id=1, source_target_pairs={{8,0},{16,8},{24,16},{32,24},{40,32},{48,40},{56,48},{64,56},{72,6... | collective-permute-start | bytes 294920 | tf_op jit(solution)/shard_map/ppermute | solution.py:138
  40.0 1.9 %collective-permute-start.1 = (bf16[3,64,256]{2,1,0:T(8,128)(2,1)S(1)}, bf16[3,64,256]{2,1,0:T(8,128)(2,1)S(1)}, u32[]{:S(2)}, u32[]{:S(2)}) collective-permute-start(bf16[3,64,256]{2,1,0:T(8,128)(2,1)S(1)} %get-tuple-element.3), channel_id=1, source_target_pairs={{0,8},{8,16},{16,24},{24,32},{32,40},{40,48},{48,56},{56,64},{64,7... | collective-permute-start | bytes 294920 | tf_op jit(solution)/shard_map/ppermute | solution.py:137
  42.0 0.0 copy-done.5
  42.0 0.6 fusion.2
  42.6 0.0 copy-done.2
  42.6 0.3 copy.8
  42.8 1.1 %reshape.17.weights_ref = f32[144,1024]{1,0:T(8,128)} reshape(f32[16,3,3,1024]{3,2,1,0:T(4,128)S(1)} %copy.8) | data formatting | bytes 1179648 | tf_op jit(solution)/shard_map/reshape | solution.py:140
  44.0 0.0 collective-permute-done.2.after_ref
  44.0 0.0 copy-start.3
  44.0 5.0 %collective-permute-done.1.before_ref = bf16[3,64,256]{2,1,0:T(8,128)(2,1)S(1)} collective-permute-done((bf16[3,64,256]{2,1,0:T(8,128)(2,1)S(1)}, bf16[3,64,256]{2,1,0:T(8,128)(2,1)S(1)}, u32[]{:S(2)}, u32[]{:S(2)}) %collective-permute-start.1) | collective-permute-done | bytes 98336 | tf_op jit(solution)/shard_map/ppermute | solution.py:137
  49.0 0.0 copy-done.3
  49.0 0.0 copy-start.4
  49.0 0.6 copy-done.4
  49.6 9.5 %stencil.1.image_ref = bf16[3,64,1024]{2,1,0:T(8,128)(2,1)} custom-call(s32[16,1024]{1,0:T(8,128)} %columns_ref.1, f32[144,1024]{1,0:T(8,128)} %reshape.17.weights_ref, bf16[3,64,256]{2,1,0:T(8,128)(2,1)} %copy-done.4, bf16[3,64,1024]{2,1,0:T(8,128)(2,1)} %basis_ref.1, bf16[3,64,256]{2,1,0:T(8,128)(2,1)} %copy-done.3), custom_call_target="tpu_custom_call" | custom-call | tf_op jit(solution)/shard_map/stencil/pallas_call | solution.py:70
  59.1 0.0 copy-done
  59.1 2.8 %sampled.1.sampled_ref = f32[512,64]{1,0:T(8,128)} custom-call(s32[1,512]{1,0:T(1,128)} %bitcast.4, bf16[512,512]{1,0:T(8,128)(2,1)} %inverse_ref.1, bf16[3,64,1024]{2,1,0:T(8,128)(2,1)} %stencil.1.image_ref), custom_call_target="tpu_custom_call" | custom-call | tf_op jit(solution)/shard_map/sampled/pallas_call | solution.py:96
  61.9 0.0 collective-permute-done.theirs_ref
  61.9 3.7 %reduced.1 = f32[512,128]{1,0:T(8,128)} custom-call(s32[1]{0:T(128)} %bitcast.core_ref, bf16[4,3,64,1024]{3,2,1,0:T(8,128)(2,1)} %copy-done, bf16[4,3,64,1024]{3,2,1,0:T(8,128)(2,1)} %collective-permute-done.theirs_ref, bf16[3,64,1024]{2,1,0:T(8,128)(2,1)} %stencil.1.image_ref, f32[512,64]{1,0:T(8,128)} %sampled.1.sampled_ref), custom_call_target="tpu_custom_call" | custom-call | tf_op jit(solution)/shard_map/reduced/pallas_call | solution.py:120
  65.6 29.3 %all_to_all.11 = f32[64,8,128]{2,1,0:T(8,128)S(1)} all-to-all(f32[64,8,128]{2,1,0:T(8,128)} %bitcast.3), channel_id=1, replica_groups=mesh['y'=4,'z'=16,'x'=4,'core'=2] {'y','z'}, dimensions={0} | all-to-all | bytes 524288 | tf_op jit(solution)/shard_map/all_to_all | solution.py:149
  94.9 0.1 reduce_sum.9
  95.0 0.7 fusion.6
  (1 shorter events, 0.0 us)
Async XLA Ops:
  1.8 26.9 %copy-start.1 = (bf16[3,64,1024]{2,1,0:T(8,128)(2,1)S(1)}, bf16[3,64,1024]{2,1,0:T(8,128)(2,1)}, u32[]{:S(2)}) copy-start(bf16[3,64,1024]{2,1,0:T(8,128)(2,1)} %basis_ref.1) | copy-start | bytes 1179652
  1.8 40.1 %copy-start.5 = (s32[512]{0:T(512)S(1)}, s32[512]{0:T(512)}, u32[]{:S(2)}) copy-start(s32[512]{0:T(512)} %param.8) | copy-start | bytes 6148
  1.8 40.7 %copy-start.2 = (bf16[16,3,3,1024]{3,0,2,1:T(8,128)(2,1)S(1)}, bf16[16,3,3,1024]{3,0,2,1:T(8,128)(2,1)}, u32[]{:S(2)}) copy-start(bf16[16,3,3,1024]{3,0,2,1:T(8,128)(2,1)} %param.6) | copy-start | bytes 884740
  26.8 32.3 %copy-start = (bf16[4,3,64,1024]{3,2,1,0:T(8,128)(2,1)}, bf16[4,3,64,1024]{3,2,1,0:T(8,128)(2,1)S(1)}, u32[]{:S(2)}) copy-start(bf16[4,3,64,1024]{3,2,1,0:T(8,128)(2,1)S(1)} %all_to_all.10.mine_ref) | copy-start | bytes 4718596
  26.8 35.1 %collective-permute-start = (bf16[4,3,64,1024]{3,2,1,0:T(8,128)(2,1)S(1)}, bf16[4,3,64,1024]{3,2,1,0:T(8,128)(2,1)}, u32[]{:S(2)}, u32[]{:S(2)}) collective-permute-start(bf16[4,3,64,1024]{3,2,1,0:T(8,128)(2,1)S(1)} %all_to_all.10.mine_ref), channel_id=1, source_target_pairs={{0,1},{1,0},{2,3},{3,2},{4,5},{5,4},{6,7},{7,6},{8,9},{9,8},{10,11... | collective-permute-start | bytes 4718600 | tf_op jit(solution)/shard_map/ppermute | solution.py:146
  28.7 15.2 %collective-permute-start.2 = (bf16[3,64,256]{2,1,0:T(8,128)(2,1)S(1)}, bf16[3,64,256]{2,1,0:T(8,128)(2,1)S(1)}, u32[]{:S(2)}, u32[]{:S(2)}) collective-permute-start(bf16[3,64,256]{2,1,0:T(8,128)(2,1)S(1)} %get-tuple-element.2), channel_id=1, source_target_pairs={{8,0},{16,8},{24,16},{32,24},{40,32},{48,40},{56,48},{64,56},{72,6... | collective-permute-start | bytes 294920 | tf_op jit(solution)/shard_map/ppermute | solution.py:138
  40.0 8.9 %collective-permute-start.1 = (bf16[3,64,256]{2,1,0:T(8,128)(2,1)S(1)}, bf16[3,64,256]{2,1,0:T(8,128)(2,1)S(1)}, u32[]{:S(2)}, u32[]{:S(2)}) collective-permute-start(bf16[3,64,256]{2,1,0:T(8,128)(2,1)S(1)} %get-tuple-element.3), channel_id=1, source_target_pairs={{0,8},{8,16},{16,24},{24,32},{32,40},{40,48},{48,56},{56,64},{64,7... | collective-permute-start | bytes 294920 | tf_op jit(solution)/shard_map/ppermute | solution.py:137
  44.0 5.0 %copy-start.3 = (bf16[3,64,256]{2,1,0:T(8,128)(2,1)}, bf16[3,64,256]{2,1,0:T(8,128)(2,1)S(1)}, u32[]{:S(2)}) copy-start(bf16[3,64,256]{2,1,0:T(8,128)(2,1)S(1)} %collective-permute-done.2.after_ref) | copy-start | bytes 294916
  49.0 0.6 copy-start.4

commit v2 on v1

v2 whole, which is shorter than its diff:
```python
import math

import jax
import jax.numpy as jnp
from jax import lax
from jax.experimental import pallas as pl
from jax.experimental.pallas import tpu as pltpu
from jax.sharding import Mesh, PartitionSpec as P


DOM = ("y", "z")
MODE = ("x", "core")
F32 = jnp.float32
BF16 = jnp.bfloat16
LANES = 128


def in_vmem(x):
    return pltpu.with_memory_space_constraint(x, pltpu.VMEM)


PARAMS = pltpu.CompilerParams(vmem_limit_bytes=16 * 2**20)
VMEM_SPEC = pl.BlockSpec(memory_space=pltpu.VMEM)


def spread_kernel(basis_ref, copies_ref, first_ref, last_ref):
    nodes, halo = basis_ref.shape[2], first_ref.shape[2]
    for x in range(copies_ref.shape[0]):
        copies_ref[x] = basis_ref[...]
    first_ref[...] = basis_ref[:, :, :halo]
    last_ref[...] = basis_ref[:, :, nodes - halo :]


def spread(basis, chips):
    parts, modes, nodes = basis.shape
    side = pltpu.VMEM((parts, modes, nodes // 4), BF16)
    return pl.pallas_call(
        spread_kernel,
        out_shape=(pltpu.VMEM((chips, *basis.shape), BF16), side, side),
        in_specs=[VMEM_SPEC],
        out_specs=(VMEM_SPEC,) * 3,
        compiler_params=PARAMS,
        name="spread",
    )(basis)


def slot_sums(columns_ref, blocks_ref, target_ref, weights_ref, image_ref, values, here, there, halo):
    slots = columns_ref.shape[0]
    parts, modes, _ = image_ref.shape
    window = values.shape[1]
    chunks = window // LANES
    lane = lax.broadcasted_iota(jnp.int32, (slots, LANES), 1)
    row_ids = lax.broadcasted_iota(jnp.int32, (16, LANES), 0)
    one = jnp.ones((16, LANES), BF16)
    zero = jnp.zeros((16, LANES), BF16)
    ids = [(row_ids + 16 * q).astype(F32).astype(BF16) for q in range(LANES // 16)]
    offset = columns_ref[:, here]
    target = jnp.where(offset == halo + 1, -window, lane + offset + halo)
    for k in range(chunks):
        target_ref[k * slots : (k + 1) * slots, :] = jnp.clip(target - LANES * k, -1, LANES).astype(F32)
    for a in range(parts):
        for b in range(parts):
            row = (a * parts + b) * slots
            weights_ref[row : row + slots, :] = blocks_ref[a, b, :, here].astype(F32)
    sums = [jnp.zeros((modes, LANES), F32) for _ in range(parts)]
    for pair in range(slots // 2):
        both = []
        for j in (2 * pair, 2 * pair + 1):
            hits = []
            for k in range(chunks):
                row = k * slots + j
                wanted = jnp.broadcast_to(target_ref[row : row + 1, :], (16, LANES)).astype(BF16)
                hits += [jnp.where(i == wanted, one, zero) for i in ids]
            both.append(jnp.concatenate(hits, axis=0))
        picked = jnp.dot(values, jnp.concatenate(both, axis=1), preferred_element_type=F32)
        for side in range(2):
            j = 2 * pair + side
            for b in range(parts):
                nearby = picked[b * modes : (b + 1) * modes, side * LANES : (side + 1) * LANES]
                for a in range(parts):
                    row = (a * parts + b) * slots + j
                    sums[a] = sums[a] + weights_ref[row : row + 1, :] * nearby
    for a in range(parts):
        image_ref[a, :, there] = sums[a].astype(BF16)


def inner_kernel(columns_ref, blocks_ref, basis_ref, image_ref, target_ref, weights_ref):
    parts, modes, nodes = basis_ref.shape
    halo = nodes // 4
    window = LANES + 2 * halo

    def node_block(step, carry):
        first = pl.multiple_of(step * LANES, LANES)
        values = basis_ref[:, :, pl.ds(first, window)].reshape(parts * modes, window)
        here = pl.ds(pl.multiple_of(first + halo, LANES), LANES)
        slot_sums(columns_ref, blocks_ref, target_ref, weights_ref, image_ref, values, here, pl.ds(first, LANES), halo)
        return carry

    lax.fori_loop(0, (nodes - 2 * halo) // LANES, node_block, 0)


def edge_kernel(
    columns_ref, blocks_ref, before_ref, basis_ref, after_ref, inner_ref, image_ref, target_ref, weights_ref, extended_ref
):
    parts, modes, nodes = basis_ref.shape
    halo = nodes // 4
    window = LANES + 2 * halo
    for b in range(parts):
        rows = slice(b * modes, (b + 1) * modes)
        extended_ref[0, rows, 0:halo] = before_ref[b]
        extended_ref[0, rows, halo:] = basis_ref[b, :, : 2 * halo]
        extended_ref[1, rows, : 2 * halo] = basis_ref[b, :, nodes - 2 * halo :]
        extended_ref[1, rows, 2 * halo :] = after_ref[b]
        image_ref[b, :, halo : nodes - halo] = inner_ref[b]
    blocks = halo // LANES

    def node_block(step, carry):
        side = step // blocks
        local = pl.multiple_of((step % blocks) * LANES, LANES)
        values = extended_ref[side, :, pl.ds(local, window)]
        here = pl.ds(pl.multiple_of(local + side * (nodes - halo), LANES), LANES)
        slot_sums(columns_ref, blocks_ref, target_ref, weights_ref, image_ref, values, here, here, halo)
        return carry

    lax.fori_loop(0, 2 * blocks, node_block, 0)


def slot_scratch(slots, parts, halo):
    return [
        pltpu.VMEM((slots * (LANES + 2 * halo) // LANES, LANES), F32),
        pltpu.VMEM((parts * parts * slots, LANES), F32),
    ]


def cost(flops, nbytes):
    return pl.CostEstimate(flops=flops, transcendentals=0, bytes_accessed=nbytes)


def inner(columns, blocks, basis):
    slots, nodes = columns.shape
    parts, modes, _ = basis.shape
    return pl.pallas_call(
        inner_kernel,
        out_shape=pltpu.VMEM((parts, modes, nodes // 2), BF16),
        in_specs=[VMEM_SPEC] * 3,
        out_specs=VMEM_SPEC,
        scratch_shapes=slot_scratch(slots, parts, nodes // 4),
        cost_estimate=cost(4 * 10**9, 2 * 10**6),
        compiler_params=PARAMS,
        name="inner",
    )(columns, blocks, in_vmem(basis))


def edges(columns, blocks, before, basis, after, inner_image):
    slots, _ = columns.shape
    parts, modes, halo = before.shape
    return pl.pallas_call(
        edge_kernel,
        out_shape=pltpu.VMEM(basis.shape, BF16),
        out_specs=VMEM_SPEC,
        scratch_shapes=slot_scratch(slots, parts, halo) + [pltpu.VMEM((2, parts * modes, 3 * halo), BF16)],
        cost_estimate=cost(4 * 10**9, 2 * 10**6),
        in_specs=[VMEM_SPEC] * 6,
        compiler_params=PARAMS,
        name="edges",
    )(columns, blocks, in_vmem(before), in_vmem(basis), in_vmem(after), in_vmem(inner_image))


def sampled_kernel(place_ref, inverse_ref, image_ref, out_ref):
    parts, modes, nodes = image_ref.shape
    samples = place_ref.shape[1]
    row_ids = lax.broadcasted_iota(jnp.int32, (16, samples), 0)
    one = jnp.ones((16, samples), BF16)
    zero = jnp.zeros((16, samples), BF16)
    ids = [(row_ids + 16 * q).astype(F32).astype(BF16) for q in range(LANES // 16)]
    place = jnp.broadcast_to(place_ref[...], (16, samples))
    total = jnp.zeros((modes, samples), F32)
    for c in range(parts):
        hits = []
        for first in range(0, nodes, LANES):
            wanted = jnp.clip(place - (c * nodes + first), -1, LANES).astype(F32).astype(BF16)
            hits += [jnp.where(i == wanted, one, zero) for i in ids]
        total = total + jnp.dot(image_ref[c], jnp.concatenate(hits, axis=0), preferred_element_type=F32)
    out_ref[:, 0:modes] = jnp.zeros((inverse_ref.shape[0], modes), F32)
    out_ref[:, modes:] = lax.dot_general(
        inverse_ref[...], total.astype(BF16), (((1,), (1,)), ((), ())), preferred_element_type=F32
    )


def sampled(place, inverse, image):
    return pl.pallas_call(
        sampled_kernel,
        in_specs=[VMEM_SPEC] * 3,
        out_shape=jax.ShapeDtypeStruct((inverse.shape[0], 2 * image.shape[1]), F32),
        cost_estimate=cost(2 * 10**9, 2 * 10**6),
        compiler_params=PARAMS,
        name="sampled",
    )(place, inverse, in_vmem(image))


def reduced_kernel(core_ref, basis_ref, image_ref, rest_ref, out_ref):
    chips, parts, modes, nodes = basis_ref.shape
    out_ref[...] = rest_ref[...]
    total = jnp.zeros((chips * modes, modes), F32)
    for c in range(parts):
        total = total + lax.dot_general(
            basis_ref[:, c].reshape(chips * modes, nodes), image_ref[c], (((1,), (1,)), ((), ())), preferred_element_type=F32
        )
    for x in range(chips):
        first = pl.multiple_of((2 * x + core_ref[0]) * modes, modes)
        out_ref[pl.ds(first, modes), 0:modes] = total[x * modes : (x + 1) * modes]


def reduced_rows(core, basis, image, rest):
    return pl.pallas_call(
        reduced_kernel,
        in_specs=[pl.BlockSpec(memory_space=pltpu.SMEM)] + [VMEM_SPEC] * 3,
        out_specs=VMEM_SPEC,
        out_shape=pltpu.VMEM(rest.shape, F32),
        cost_estimate=cost(2 * 10**9, 2 * 10**6),
        compiler_params=PARAMS,
        name="reduced",
    )(core, in_vmem(basis), in_vmem(image), rest)


def shards(mode_basis, blocks, columns, samples, inverse):
    parts, modes, node_count = mode_basis.shape
    chips = lax.axis_size("x")
    doms = lax.axis_size(DOM)
    dom = lax.axis_index(DOM)
    copies, first, last = spread(mode_basis, chips)
    mine = lax.all_to_all(copies, "x", 0, 0)
    before = lax.ppermute(last, DOM, [(i, (i + 1) % doms) for i in range(doms)])
    after = lax.ppermute(first, DOM, [((i + 1) % doms, i) for i in range(doms)])
    blocks = jnp.transpose(blocks, (1, 2, 0, 3))
    inner_image = inner(columns, blocks, mode_basis)
    image = edges(columns, blocks, before, mode_basis, after, inner_image)
    node = samples // 3 - dom * node_count
    owned = (node >= 0) & (node < node_count)
    place = jnp.where(owned, (samples % 3) * node_count + node, -1)[None]
    theirs = lax.ppermute(mine, "core", [(0, 1), (1, 0)])
    partial = sampled(place, inverse, image)
    core = lax.axis_index("core").astype(jnp.int32)[None]
    partial = reduced_rows(core, mine, image, partial)
    partial = reduced_rows(1 - core, theirs, image, in_vmem(partial))
    pieces = lax.all_to_all(partial.reshape(doms, -1, 2 * modes), DOM, 0, 0)
    total = jnp.sum(pieces, axis=0)
    scaling = 1.0 / math.sqrt(parts * node_count * doms)
    return total[:, :modes] * scaling, total[:, modes:]


def solution(mesh):
    step_mesh = Mesh(mesh.devices.reshape(4, 16, 4, 2), DOM + MODE)

    return jax.shard_map(
        shards,
        mesh=step_mesh,
        in_specs=(P(None, MODE, DOM), P(None, None, None, DOM), P(None, DOM), P(), P()),
        out_specs=(P(DOM, MODE), P(DOM, MODE)),
        check_vma=False,
    )
```

time: 96 us -> 93.3 us (0.972)
  waiting for transfers between devices: 4.99 us -> 0.01 us
  Pallas kernels: 16 us -> 11.7 us
  blocking collectives: 54.2 us -> 58.2 us
  local copies, waits for them, and re-layouts: 3.24 us -> 6.25 us
    unnamed x12 -> x20, local copies, waits for them, and re-layouts: 0.66 us -> 6.25 us
    ppermute x2, waiting for transfers between devices: 4.98 us -> 0.01 us  [the longest x1 0.01 us: shards(): before = lax.ppermute(last, DOM, [(i, (i + 1) % doms) for i in range(doms)])]
    all_to_all x1, blocking collectives: 29.3 us -> 33.3 us  [shards(): pieces = lax.all_to_all(partial.reshape(doms, -1, 2 * modes), DOM, 0, 0)]
    pallas_call x1 -> x2, Pallas kernels: 3.72 us -> 1.11 us  [reduced_rows(): pl.pallas_call(reduced_kernel, in_specs=[pl.BlockSpec(memory_space=pltpu....]
    pallas_call x2 -> x4, Pallas kernels: 12.3 us -> 10.6 us  [the longest x1 4.93 us: edges(): pl.pallas_call(edge_kernel, out_shape=pltpu.VMEM(basis.shape, BF16), out_...]
    reshape x2 -> x0, local copies, waits for them, and re-layouts: 1.39 us -> none  [shards(): weights = blocks.astype(F32).reshape(-1, node_count)]
    broadcast_in_dim x1 -> x0, local copies, waits for them, and re-layouts: 1.18 us -> none  [shards(): jnp.broadcast_to(mode_basis[None], (chips, *mode_basis.shape))]
  transfers between devices with their start and end apart: 3 -> 3, of which waited for: 1 -> 0; matrix products, arithmetic and copies ran while one was open for 2% -> 0% of each run, Pallas kernels for 13% -> 11%
where the time goes in v2:
time: 93.3 us; the launch traced here: 92.8 us
  blocking collectives  58.2 us (62%)
  starting transfers between devices  15.1 us (16%)
  Pallas kernels  11.7 us (13%)
  local copies, waits for them, and re-layouts  6.25 us (7%)
    all_to_all x1, blocking collectives, shards(): pieces = lax.all_to_all(partial.reshape(doms, -1, 2 * modes), DOM, 0, 0)  33.3 us
    all_to_all x1, blocking collectives, shards(): mine = lax.all_to_all(copies, 'x', 0, 0)  24.9 us
    ppermute x1, starting transfers between devices, shards(): after = lax.ppermute(first, DOM, [((i + 1) % doms, i) for i in range(doms)])  9.38 us
    unnamed x20, local copies, waits for them, and re-layouts  6.25 us
    pallas_call x1, Pallas kernels, edges(): pl.pallas_call(edge_kernel, out_shape=pltpu.VMEM(basis.shape, BF16), out_...  4.93 us
    pallas_call x1, Pallas kernels, inner(): pl.pallas_call(inner_kernel, out_shape=pltpu.VMEM((parts, modes, nodes //...  3.9 us
    ppermute x1, starting transfers between devices, shards(): before = lax.ppermute(last, DOM, [(i, (i + 1) % doms) for i in range(doms)])  3.83 us
    ppermute x1, starting transfers between devices, shards(): theirs = lax.ppermute(mine, 'core', [(0, 1), (1, 0)])  1.91 us
  transfers between devices with their start and end apart: 3, of which 0 were waited for; matrix products, arithmetic and copies ran while one was open for 0% of the time, Pallas kernels for 11%

profile of v2, /device:TPU:8, one launch (start us, length us, event | category | flops | bytes accessed | tf_op | source)
XLA Modules:
  0.0 92.8 jit_solution(105145047061751109)
XLA Ops:
  0.6 0.0 copy-start
  0.6 1.0 %copy-done = bf16[3,64,1024]{2,1,0:T(8,128)(2,1)S(1)} copy-done((bf16[3,64,1024]{2,1,0:T(8,128)(2,1)S(1)}, bf16[3,64,1024]{2,1,0:T(8,128)(2,1)}, u32[]{:S(2)}) %copy-start) | copy-done | bytes 393240
  1.6 0.8 spread.1
  2.4 0.0 copy-start.1
  2.4 24.9 %all_to_all.10.basis_ref = bf16[4,3,64,1024]{3,2,1,0:T(8,128)(2,1)S(1)} all-to-all(bf16[4,3,64,1024]{3,2,1,0:T(8,128)(2,1)S(1)} %get-tuple-element.5), channel_id=1, replica_groups=mesh['y'=4,'z'=16,'x'=4,'core'=2] {'x'}, dimensions={0} | all-to-all | bytes 3145728 | tf_op jit(solution)/shard_map/all_to_all | solution.py:232
  27.3 1.9 %collective-permute-start = (bf16[4,3,64,1024]{3,2,1,0:T(8,128)(2,1)S(1)}, bf16[4,3,64,1024]{3,2,1,0:T(8,128)(2,1)S(1)}, u32[]{:S(2)}, u32[]{:S(2)}) collective-permute-start(bf16[4,3,64,1024]{3,2,1,0:T(8,128)(2,1)S(1)} %all_to_all.10.basis_ref), channel_id=1, source_target_pairs={{0,1},{1,0},{2,3},{3,2},{4,5},{5,4},{6,7},{7,6},{8,9},{9,8},{10,11... | collective-permute-start | bytes 4718600 | tf_op jit(solution)/shard_map/ppermute | solution.py:241
  29.3 3.8 %collective-permute-start.1 = (bf16[3,64,256]{2,1,0:T(8,128)(2,1)}, bf16[3,64,256]{2,1,0:T(8,128)(2,1)}, u32[]{:S(2)}, u32[]{:S(2)}) collective-permute-start(bf16[3,64,256]{2,1,0:T(8,128)(2,1)} %get-tuple-element.6), channel_id=1, source_target_pairs={{0,8},{8,16},{16,24},{24,32},{32,40},{40,48},{48,56},{56,64},{64,7... | collective-permute-start | bytes 294920 | tf_op jit(solution)/shard_map/ppermute | solution.py:233
  33.1 9.4 %collective-permute-start.2 = (bf16[3,64,256]{2,1,0:T(8,128)(2,1)}, bf16[3,64,256]{2,1,0:T(8,128)(2,1)}, u32[]{:S(2)}, u32[]{:S(2)}) collective-permute-start(bf16[3,64,256]{2,1,0:T(8,128)(2,1)} %get-tuple-element.7), channel_id=1, source_target_pairs={{8,0},{16,8},{24,16},{32,24},{40,32},{48,40},{56,48},{64,56},{72,6... | collective-permute-start | bytes 294920 | tf_op jit(solution)/shard_map/ppermute | solution.py:234
  42.5 0.0 copy-done.1
  42.5 0.0 copy-start.3
  42.5 1.0 %copy-done.3 = bf16[16,3,3,1024]{3,0,2,1:T(8,128)(2,1)S(1)} copy-done((bf16[16,3,3,1024]{3,0,2,1:T(8,128)(2,1)S(1)}, bf16[16,3,3,1024]{3,0,2,1:T(8,128)(2,1)}, u32[]{:S(2)}) %copy-start.3) | copy-done | bytes 294936
  43.5 0.0 copy-start.5
  43.5 0.8 copy-done.5
  44.3 0.0 copy-start.9
  44.3 3.9 %inner.1.inner_ref = bf16[3,64,512]{2,1,0:T(8,128)(2,1)S(1)} custom-call(s32[16,1024]{1,0:T(8,128)S(1)} %copy-done.5, bf16[3,3,16,1024]{3,2,1,0:T(8,128)(2,1)S(1)} %bitcast.6, bf16[3,64,1024]{2,1,0:T(8,128)(2,1)S(1)} %copy-done.1), custom_call_target="tpu_custom_call" | custom-call | flops 4000000000 | bytes 2000000 | tf_op jit(solution)/shard_map/inner/pallas_call | solution.py:142
  48.2 0.0 copy-start.7
  48.2 0.7 copy-done.7
  48.9 0.0 copy-done.9
  48.9 0.0 copy-start.2
  48.9 0.0 collective-permute-done.1.before_ref
  48.9 0.0 collective-permute-done.2.after_ref
  49.0 0.0 copy-start.4
  49.0 1.0 %copy-done.4 = bf16[16,3,3,1024]{3,0,2,1:T(8,128)(2,1)S(1)} copy-done((bf16[16,3,3,1024]{3,0,2,1:T(8,128)(2,1)S(1)}, bf16[16,3,3,1024]{3,0,2,1:T(8,128)(2,1)}, u32[]{:S(2)}) %copy-start.4) | copy-done | bytes 294936
  50.0 0.0 copy-start.6
  50.0 0.8 copy-done.6
  50.8 0.0 copy-start.8
  50.8 0.9 copy-done.8
  51.7 4.9 %edges.1.image_ref = bf16[3,64,1024]{2,1,0:T(8,128)(2,1)S(1)} custom-call(s32[16,1024]{1,0:T(8,128)S(1)} %copy-done.6, bf16[3,3,16,1024]{3,2,1,0:T(8,128)(2,1)S(1)} %bitcast.7, bf16[3,64,256]{2,1,0:T(8,128)(2,1)} %collective-permute-done.1.before_ref, bf16[3,64,1024]{2,1,0:T(8,128)(2,1)S(1)} %copy-done.1, ...), custom_call_target="tpu_custom_call" | custom-call | flops 4000000000 | bytes 2000000 | tf_op jit(solution)/shard_map/edges/pallas_call | solution.py:157
  56.7 0.0 copy-done.2
  56.7 1.0 %sampled.1.rest_ref = f32[512,128]{1,0:T(8,128)S(1)} custom-call(s32[1,512]{1,0:T(1,128)S(1)} %bitcast.5, bf16[512,512]{1,0:T(8,128)(2,1)S(1)} %copy-done.2, bf16[3,64,1024]{2,1,0:T(8,128)(2,1)S(1)} %edges.1.image_ref), custom_call_target="tpu_custom_call" | custom-call | flops 2000000000 | bytes 2000000 | tf_op jit(solution)/shard_map/sampled/pallas_call | solution.py:191
  57.7 0.6 reduced.2.rest_ref
  58.3 0.0 collective-permute-done.basis_ref
  58.3 0.6 reduced.3
  58.8 33.3 %all_to_all.11 = f32[64,8,128]{2,1,0:T(8,128)S(1)} all-to-all(f32[64,8,128]{2,1,0:T(8,128)S(1)} %bitcast.4), channel_id=1, replica_groups=mesh['y'=4,'z'=16,'x'=4,'core'=2] {'y','z'}, dimensions={0} | all-to-all | bytes 524288 | tf_op jit(solution)/shard_map/all_to_all | solution.py:246
  92.1 0.1 reduce_sum.9
  92.2 0.7 fusion.5
  (1 shorter events, 0.0 us)
Async XLA Ops:
  0.6 1.0 %copy-start = (bf16[3,64,1024]{2,1,0:T(8,128)(2,1)S(1)}, bf16[3,64,1024]{2,1,0:T(8,128)(2,1)}, u32[]{:S(2)}) copy-start(bf16[3,64,1024]{2,1,0:T(8,128)(2,1)} %basis_ref.5) | copy-start | bytes 1179652
  2.4 40.1 %copy-start.1 = (bf16[3,64,1024]{2,1,0:T(8,128)(2,1)S(1)}, bf16[3,64,1024]{2,1,0:T(8,128)(2,1)}, u32[]{:S(2)}) copy-start(bf16[3,64,1024]{2,1,0:T(8,128)(2,1)} %basis_ref.5) | copy-start | bytes 1179652
  27.3 30.9 %collective-permute-start = (bf16[4,3,64,1024]{3,2,1,0:T(8,128)(2,1)S(1)}, bf16[4,3,64,1024]{3,2,1,0:T(8,128)(2,1)S(1)}, u32[]{:S(2)}, u32[]{:S(2)}) collective-permute-start(bf16[4,3,64,1024]{3,2,1,0:T(8,128)(2,1)S(1)} %all_to_all.10.basis_ref), channel_id=1, source_target_pairs={{0,1},{1,0},{2,3},{3,2},{4,5},{5,4},{6,7},{7,6},{8,9},{9,8},{10,11... | collective-permute-start | bytes 4718600 | tf_op jit(solution)/shard_map/ppermute | solution.py:241
  29.3 19.7 %collective-permute-start.1 = (bf16[3,64,256]{2,1,0:T(8,128)(2,1)}, bf16[3,64,256]{2,1,0:T(8,128)(2,1)}, u32[]{:S(2)}, u32[]{:S(2)}) collective-permute-start(bf16[3,64,256]{2,1,0:T(8,128)(2,1)} %get-tuple-element.6), channel_id=1, source_target_pairs={{0,8},{8,16},{16,24},{24,32},{32,40},{40,48},{48,56},{56,64},{64,7... | collective-permute-start | bytes 294920 | tf_op jit(solution)/shard_map/ppermute | solution.py:233
  33.1 15.8 %collective-permute-start.2 = (bf16[3,64,256]{2,1,0:T(8,128)(2,1)}, bf16[3,64,256]{2,1,0:T(8,128)(2,1)}, u32[]{:S(2)}, u32[]{:S(2)}) collective-permute-start(bf16[3,64,256]{2,1,0:T(8,128)(2,1)} %get-tuple-element.7), channel_id=1, source_target_pairs={{8,0},{16,8},{24,16},{32,24},{40,32},{48,40},{56,48},{64,56},{72,6... | collective-permute-start | bytes 294920 | tf_op jit(solution)/shard_map/ppermute | solution.py:234
  42.5 1.0 %copy-start.3 = (bf16[16,3,3,1024]{3,0,2,1:T(8,128)(2,1)S(1)}, bf16[16,3,3,1024]{3,0,2,1:T(8,128)(2,1)}, u32[]{:S(2)}) copy-start(bf16[16,3,3,1024]{3,0,2,1:T(8,128)(2,1)} %param.6) | copy-start | bytes 884740
  43.5 0.8 copy-start.5
  44.3 4.6 %copy-start.9 = (s32[512]{0:T(512)S(1)}, s32[512]{0:T(512)}, u32[]{:S(2)}) copy-start(s32[512]{0:T(512)} %param.8) | copy-start | bytes 6148
  48.2 0.7 copy-start.7
  48.9 7.8 %copy-start.2 = (bf16[512,512]{1,0:T(8,128)(2,1)S(1)}, bf16[512,512]{1,0:T(8,128)(2,1)}, u32[]{:S(2)}) copy-start(bf16[512,512]{1,0:T(8,128)(2,1)} %inverse_ref.1) | copy-start | bytes 1572868
  49.0 1.0 %copy-start.4 = (bf16[16,3,3,1024]{3,0,2,1:T(8,128)(2,1)S(1)}, bf16[16,3,3,1024]{3,0,2,1:T(8,128)(2,1)}, u32[]{:S(2)}) copy-start(bf16[16,3,3,1024]{3,0,2,1:T(8,128)(2,1)} %param.6) | copy-start | bytes 884740
  50.0 0.8 copy-start.6
  50.8 0.9 copy-start.8

commit v3 on v2

--- a/solution.py
+++ b/solution.py
@@ -1,3 +1,4 @@
+import functools
 import math
 
 import jax
@@ -13,6 +14,7 @@
 F32 = jnp.float32
 BF16 = jnp.bfloat16
 LANES = 128
+TRAVEL = BF16
 
 
 def in_vmem(x):
@@ -55,9 +57,9 @@
     zero = jnp.zeros((16, LANES), BF16)
     ids = [(row_ids + 16 * q).astype(F32).astype(BF16) for q in range(LANES // 16)]
     offset = columns_ref[:, here]
-    target = jnp.where(offset == halo + 1, -window, lane + offset + halo)
-    for k in range(chunks):
-        target_ref[k * slots : (k + 1) * slots, :] = jnp.clip(target - LANES * k, -1, LANES).astype(F32)
+    target = jnp.where(offset == halo + 1, -LANES, lane + offset + halo)
+    target_ref[:slots, :] = (target & (LANES - 1)).astype(F32)
+    target_ref[slots:, :] = (target >> (LANES.bit_length() - 1)).astype(F32)
     for a in range(parts):
         for b in range(parts):
             row = (a * parts + b) * slots
@@ -66,11 +68,13 @@
     for pair in range(slots // 2):
         both = []
         for j in (2 * pair, 2 * pair + 1):
+            lower = jnp.broadcast_to(target_ref[j : j + 1, :], (16, LANES)).astype(BF16)
+            upper = jnp.broadcast_to(target_ref[slots + j : slots + j + 1, :], (16, LANES)).astype(BF16)
+            ones = [jnp.where(i == lower, one, zero) for i in ids]
             hits = []
             for k in range(chunks):
-                row = k * slots + j
-                wanted = jnp.broadcast_to(target_ref[row : row + 1, :], (16, LANES)).astype(BF16)
-                hits += [jnp.where(i == wanted, one, zero) for i in ids]
+                inside = upper == jnp.full((16, LANES), k, BF16)
+                hits += [jnp.where(inside, hit, zero) for hit in ones]
             both.append(jnp.concatenate(hits, axis=0))
         picked = jnp.dot(values, jnp.concatenate(both, axis=1), preferred_element_type=F32)
         for side in range(2):
@@ -89,14 +93,16 @@
     halo = nodes // 4
     window = LANES + 2 * halo
 
-    def node_block(step, carry):
-        first = pl.multiple_of(step * LANES, LANES)
-        values = basis_ref[:, :, pl.ds(first, window)].reshape(parts * modes, window)
-        here = pl.ds(pl.multiple_of(first + halo, LANES), LANES)
-        slot_sums(columns_ref, blocks_ref, target_ref, weights_ref, image_ref, values, here, pl.ds(first, LANES), halo)
+    def node_blocks(step, carry):
+        for k in range(2):
+            first = pl.multiple_of((2 * step + k) * LANES, LANES)
+            values = basis_ref[:, :, pl.ds(first, window)].reshape(parts * modes, window)
+            here = pl.ds(pl.multiple_of(first + halo, LANES), LANES)
+            scratch = (target_ref.at[k], weights_ref.at[k])
+            slot_sums(columns_ref, blocks_ref, *scratch, image_ref, values, here, pl.ds(first, LANES), halo)
         return carry
 
-    lax.fori_loop(0, (nodes - 2 * halo) // LANES, node_block, 0)
+    lax.fori_loop(0, (nodes - 2 * halo) // (2 * LANES), node_blocks, 0)
 
 
 def edge_kernel(
@@ -112,23 +118,23 @@
         extended_ref[1, rows, : 2 * halo] = basis_ref[b, :, nodes - 2 * halo :]
         extended_ref[1, rows, 2 * halo :] = after_ref[b]
         image_ref[b, :, halo : nodes - halo] = inner_ref[b]
-    blocks = halo // LANES
-
-    def node_block(step, carry):
-        side = step // blocks
-        local = pl.multiple_of((step % blocks) * LANES, LANES)
-        values = extended_ref[side, :, pl.ds(local, window)]
-        here = pl.ds(pl.multiple_of(local + side * (nodes - halo), LANES), LANES)
-        slot_sums(columns_ref, blocks_ref, target_ref, weights_ref, image_ref, values, here, here, halo)
+
+    def node_blocks(step, carry):
+        local = pl.multiple_of(step * LANES, LANES)
+        for side in range(2):
+            values = extended_ref[side, :, pl.ds(local, window)]
+            here = pl.ds(pl.multiple_of(local + side * (nodes - halo), LANES), LANES)
+            scratch = (target_ref.at[side], weights_ref.at[side])
+            slot_sums(columns_ref, blocks_ref, *scratch, image_ref, values, here, here, halo)
         return carry
 
-    lax.fori_loop(0, 2 * blocks, node_block, 0)
-
-
-def slot_scratch(slots, parts, halo):
+    lax.fori_loop(0, halo // LANES, node_blocks, 0)
+
+
+def slot_scratch(slots, parts):
     return [
-        pltpu.VMEM((slots * (LANES + 2 * halo) // LANES, LANES), F32),
-        pltpu.VMEM((parts * parts * slots, LANES), F32),
+        pltpu.VMEM((2, 2 * slots, LANES), F32),
+        pltpu.VMEM((2, parts * parts * slots, LANES), F32),
     ]
 
 
@@ -144,7 +150,7 @@
         out_shape=pltpu.VMEM((parts, modes, nodes // 2), BF16),
         in_specs=[VMEM_SPEC] * 3,
         out_specs=VMEM_SPEC,
-        scratch_shapes=slot_scratch(slots, parts, nodes // 4),
+        scratch_shapes=slot_scratch(slots, parts),
         cost_estimate=cost(4 * 10**9, 2 * 10**6),
         compiler_params=PARAMS,
         name="inner",
@@ -158,7 +164,7 @@
         edge_kernel,
         out_shape=pltpu.VMEM(basis.shape, BF16),
         out_specs=VMEM_SPEC,
-        scratch_shapes=slot_scratch(slots, parts, halo) + [pltpu.VMEM((2, parts * modes, 3 * halo), BF16)],
+        scratch_shapes=slot_scratch(slots, parts) + [pltpu.VMEM((2, parts * modes, 3 * halo), BF16)],
         cost_estimate=cost(4 * 10**9, 2 * 10**6),
         in_specs=[VMEM_SPEC] * 6,
         compiler_params=PARAMS,
@@ -181,8 +187,7 @@
             wanted = jnp.clip(place - (c * nodes + first), -1, LANES).astype(F32).astype(BF16)
             hits += [jnp.where(i == wanted, one, zero) for i in ids]
         total = total + jnp.dot(image_ref[c], jnp.concatenate(hits, axis=0), preferred_element_type=F32)
-    out_ref[:, 0:modes] = jnp.zeros((inverse_ref.shape[0], modes), F32)
-    out_ref[:, modes:] = lax.dot_general(
+    out_ref[...] = lax.dot_general(
         inverse_ref[...], total.astype(BF16), (((1,), (1,)), ((), ())), preferred_element_type=F32
     )
 
@@ -191,36 +196,79 @@
     return pl.pallas_call(
         sampled_kernel,
         in_specs=[VMEM_SPEC] * 3,
-        out_shape=jax.ShapeDtypeStruct((inverse.shape[0], 2 * image.shape[1]), F32),
+        out_shape=pltpu.VMEM((inverse.shape[0], image.shape[1]), F32),
+        out_specs=VMEM_SPEC,
         cost_estimate=cost(2 * 10**9, 2 * 10**6),
         compiler_params=PARAMS,
         name="sampled",
     )(place, inverse, in_vmem(image))
 
 
-def reduced_kernel(core_ref, basis_ref, image_ref, rest_ref, out_ref):
+def reduced_kernel(basis_ref, mine_ref, theirs_ref, kept_ref, sent_ref):
     chips, parts, modes, nodes = basis_ref.shape
-    out_ref[...] = rest_ref[...]
-    total = jnp.zeros((chips * modes, modes), F32)
-    for c in range(parts):
-        total = total + lax.dot_general(
-            basis_ref[:, c].reshape(chips * modes, nodes), image_ref[c], (((1,), (1,)), ((), ())), preferred_element_type=F32
-        )
-    for x in range(chips):
-        first = pl.multiple_of((2 * x + core_ref[0]) * modes, modes)
-        out_ref[pl.ds(first, modes), 0:modes] = total[x * modes : (x + 1) * modes]
-
-
-def reduced_rows(core, basis, image, rest):
+    for image_ref, out_ref in ((mine_ref, kept_ref), (theirs_ref, sent_ref)):
+        total = jnp.zeros((chips * modes, modes), F32)
+        for c in range(parts):
+            rows = basis_ref[:, c].reshape(chips * modes, nodes)
+            total = total + lax.dot_general(rows, image_ref[c], (((1,), (1,)), ((), ())), preferred_element_type=F32)
+        out_ref[...] = total
+
+
+def reduced_rows(basis, mine, theirs):
+    chips, _, modes, _ = basis.shape
+    out = pltpu.VMEM((chips * modes, modes), F32)
     return pl.pallas_call(
         reduced_kernel,
+        in_specs=[VMEM_SPEC] * 3,
+        out_shape=(out, out),
+        out_specs=(VMEM_SPEC, VMEM_SPEC),
+        cost_estimate=cost(2 * 10**9, 2 * 10**6),
+        compiler_params=PARAMS,
+        name="reduced",
+    )(in_vmem(basis), in_vmem(mine), in_vmem(theirs))
+
+
+def joined_kernel(core_ref, kept_ref, received_ref, sampled_ref, out_ref):
+    modes = kept_ref.shape[1]
+    core = core_ref[0]
+    for x in range(kept_ref.shape[0] // modes):
+        rows = slice(x * modes, (x + 1) * modes)
+        for source, left in ((core, kept_ref[rows, :]), (1 - core, received_ref[1 - core, rows, :])):
+            first = pl.multiple_of((2 * x + source) * modes, modes)
+            right = sampled_ref[pl.ds(first, modes), :]
+            out_ref[pl.ds(first, modes), :] = jnp.concatenate([left, right], axis=1).astype(out_ref.dtype)
+
+
+def joined(core, kept, received, sampled_part):
+    rows, modes = sampled_part.shape
+    return pl.pallas_call(
+        joined_kernel,
         in_specs=[pl.BlockSpec(memory_space=pltpu.SMEM)] + [VMEM_SPEC] * 3,
+        out_shape=pltpu.VMEM((rows, 2 * modes), TRAVEL),
         out_specs=VMEM_SPEC,
-        out_shape=pltpu.VMEM(rest.shape, F32),
-        cost_estimate=cost(2 * 10**9, 2 * 10**6),
-        compiler_params=PARAMS,
-        name="reduced",
-    )(core, in_vmem(basis), in_vmem(image), rest)
+        compiler_params=PARAMS,
+        name="joined",
+    )(core, in_vmem(kept), in_vmem(received), in_vmem(sampled_part))
+
+
+def total_kernel(scaling, pieces_ref, reduced_ref, coefficients_ref):
+    modes = reduced_ref.shape[1]
+    total = jnp.sum(pieces_ref[...].astype(F32), axis=0)
+    reduced_ref[...] = total[:, :modes] * scaling
+    coefficients_ref[...] = total[:, modes:]
+
+
+def totals(pieces, scaling):
+    _, rows, columns = pieces.shape
+    out = jax.ShapeDtypeStruct((rows, columns // 2), F32)
+    return pl.pallas_call(
+        functools.partial(total_kernel, scaling),
+        in_specs=[VMEM_SPEC],
+        out_shape=(out, out),
+        out_specs=(VMEM_SPEC, VMEM_SPEC),
+        compiler_params=PARAMS,
+        name="totals",
+    )(in_vmem(pieces))
 
 
 def shards(mode_basis, blocks, columns, samples, inverse):
@@ -238,15 +286,15 @@
     node = samples // 3 - dom * node_count
     owned = (node >= 0) & (node < node_count)
     place = jnp.where(owned, (samples % 3) * node_count + node, -1)[None]
-    theirs = lax.ppermute(mine, "core", [(0, 1), (1, 0)])
-    partial = sampled(place, inverse, image)
+    pair = [(0, 1), (1, 0)]
+    other_image = lax.ppermute(image, "core", pair)
+    sampled_part = sampled(place, inverse, image)
     core = lax.axis_index("core").astype(jnp.int32)[None]
-    partial = reduced_rows(core, mine, image, partial)
-    partial = reduced_rows(1 - core, theirs, image, in_vmem(partial))
+    kept, sent = reduced_rows(mine, image, other_image)
+    received = lax.all_gather(sent, "core")
+    partial = joined(core, kept, received, sampled_part)
     pieces = lax.all_to_all(partial.reshape(doms, -1, 2 * modes), DOM, 0, 0)
-    total = jnp.sum(pieces, axis=0)
-    scaling = 1.0 / math.sqrt(parts * node_count * doms)
-    return total[:, :modes] * scaling, total[:, modes:]
+    return totals(pieces, 1.0 / math.sqrt(parts * node_count * doms))
 
 
 def solution(mesh):

time: 93.3 us -> 66.6 us (0.71)
  blocking collectives: 58.2 us -> 33 us
  local copies, waits for them, and re-layouts: 6.25 us -> 1.01 us
  starting transfers between devices: 15.1 us -> 19.5 us
    all_to_all x1 -> x0, blocking collectives: 24.9 us -> none  [shards(): mine = lax.all_to_all(copies, 'x', 0, 0)]
    unnamed x20 -> x12, local copies, waits for them, and re-layouts: 6.25 us -> 1.01 us
    all_to_all x0 -> x1, starting transfers between devices: none -> 4.42 us  [shards(): mine = lax.all_to_all(copies, 'x', 0, 0)]
    all_to_all x1, blocking collectives: 33.3 us -> 31 us  [shards(): pieces = lax.all_to_all(partial.reshape(doms, -1, 2 * modes), DOM, 0, 0)]
    all_gather x0 -> x1, blocking collectives: none -> 1.99 us  [shards(): received = lax.all_gather(sent, 'core')]
    pallas_call x1, Pallas kernels: 4.93 us -> 3.61 us  [edges(): pl.pallas_call(edge_kernel, out_shape=pltpu.VMEM(basis.shape, BF16), out_...]
    pallas_call x3 -> x4, Pallas kernels: 2.12 us -> 2.72 us  [the longest x1 0.95 us: reduced_rows(): pl.pallas_call(reduced_kernel, in_specs=[VMEM_SPEC] * 3, out_shape=(out,...]
  transfers between devices with their start and end apart: 3 -> 4, of which waited for: 0 -> 1; matrix products, arithmetic and copies ran while one was open for 0% -> 0% of each run, Pallas kernels for 11% -> 12%
where the time goes in v3:
time: 66.6 us; the launch traced here: 66.2 us
  blocking collectives  33 us (50%)
  starting transfers between devices  19.5 us (29%)
  Pallas kernels  11.2 us (17%)
  local copies, waits for them, and re-layouts  1.01 us (2%)
  between operations  0.79 us (1%)
  waiting for transfers between devices  0.71 us (1%)
    all_to_all x1, blocking collectives, shards(): pieces = lax.all_to_all(partial.reshape(doms, -1, 2 * modes), DOM, 0, 0)  31 us
    ppermute x1, starting transfers between devices, shards(): after = lax.ppermute(first, DOM, [((i + 1) % doms, i) for i in range(doms)])  9.38 us
    all_to_all x1, starting transfers between devices, shards(): mine = lax.all_to_all(copies, 'x', 0, 0)  4.42 us
    ppermute x1, starting transfers between devices, shards(): before = lax.ppermute(last, DOM, [(i, (i + 1) % doms) for i in range(doms)])  3.81 us
    pallas_call x1, Pallas kernels, edges(): pl.pallas_call(edge_kernel, out_shape=pltpu.VMEM(basis.shape, BF16), out_...  3.61 us
    pallas_call x1, Pallas kernels, inner(): pl.pallas_call(inner_kernel, out_shape=pltpu.VMEM((parts, modes, nodes //...  3.59 us
    all_gather x1, blocking collectives, shards(): received = lax.all_gather(sent, 'core')  1.99 us
    ppermute x1, starting transfers between devices, shards(): other_image = lax.ppermute(image, 'core', pair)  1.92 us
  transfers between devices with their start and end apart: 4, of which 1 were waited for; matrix products, arithmetic and copies ran while one was open for 0% of the time, Pallas kernels for 12%

profile of v3, /device:TPU:8, one launch (start us, length us, event | category | flops | bytes accessed | tf_op | source)
XLA Modules:
  0.0 66.2 jit_solution(4095540006255451303)
XLA Ops:
  0.6 0.0 copy-start
  0.6 1.0 %copy-done = bf16[3,64,1024]{2,1,0:T(8,128)(2,1)S(1)} copy-done((bf16[3,64,1024]{2,1,0:T(8,128)(2,1)S(1)}, bf16[3,64,1024]{2,1,0:T(8,128)(2,1)}, u32[]{:S(2)}) %copy-start) | copy-done | bytes 393240
  1.6 1.3 %spread.1 = (bf16[4,3,64,1024]{3,2,1,0:T(8,128)(2,1)}, bf16[3,64,256]{2,1,0:T(8,128)(2,1)S(1)}, bf16[3,64,256]{2,1,0:T(8,128)(2,1)S(1)}) custom-call(bf16[3,64,1024]{2,1,0:T(8,128)(2,1)S(1)} %copy-done), custom_call_target="tpu_custom_call" | custom-call | tf_op jit(solution)/shard_map/spread/pallas_call | solution.py:39
  2.9 0.0 copy-start.1
  2.9 0.0 copy-start.3
  2.9 0.0 copy-start.4
  2.9 4.4 %all-to-all-start = ((bf16[4,3,64,1024]{3,2,1,0:T(8,128)(2,1)}), bf16[4,3,64,1024]{3,2,1,0:T(8,128)(2,1)S(1)}, u32[]{:S(2)}, u32[]{:S(2)}) async-start(bf16[4,3,64,1024]{3,2,1,0:T(8,128)(2,1)} %get-tuple-element.7), calls=%async_computation | async-start | bytes 3145728 | tf_op jit(solution)/shard_map/all_to_all | solution.py:280
  7.3 3.8 %collective-permute-start = (bf16[3,64,256]{2,1,0:T(8,128)(2,1)S(1)}, bf16[3,64,256]{2,1,0:T(8,128)(2,1)S(1)}, u32[]{:S(2)}, u32[]{:S(2)}) collective-permute-start(bf16[3,64,256]{2,1,0:T(8,128)(2,1)S(1)} %get-tuple-element.8), channel_id=1, source_target_pairs={{0,8},{8,16},{16,24},{24,32},{32,40},{40,48},{48,56},{56,64},{64,7... | collective-permute-start | bytes 294920 | tf_op jit(solution)/shard_map/ppermute | solution.py:281
  11.2 9.4 %collective-permute-start.1 = (bf16[3,64,256]{2,1,0:T(8,128)(2,1)S(1)}, bf16[3,64,256]{2,1,0:T(8,128)(2,1)S(1)}, u32[]{:S(2)}, u32[]{:S(2)}) collective-permute-start(bf16[3,64,256]{2,1,0:T(8,128)(2,1)S(1)} %get-tuple-element.9), channel_id=1, source_target_pairs={{8,0},{16,8},{24,16},{32,24},{40,32},{48,40},{56,48},{64,56},{72,6... | collective-permute-start | bytes 294920 | tf_op jit(solution)/shard_map/ppermute | solution.py:282
  20.6 0.0 copy-done.1
  20.6 0.0 copy-done.3
  20.6 0.0 copy-done.4
  20.6 3.6 %inner.1.inner_ref = bf16[3,64,512]{2,1,0:T(8,128)(2,1)S(1)} custom-call(s32[16,1024]{1,0:T(8,128)S(1)} %copy-done.4, bf16[3,3,16,1024]{3,2,1,0:T(8,128)(2,1)S(1)} %bitcast.8, bf16[3,64,1024]{2,1,0:T(8,128)(2,1)S(1)} %copy-done.1), custom_call_target="tpu_custom_call" | custom-call | flops 4000000000 | bytes 2000000 | tf_op jit(solution)/shard_map/inner/pallas_call | solution.py:148
  24.2 0.0 copy-start.5
  24.2 0.0 copy-start.2
  24.2 0.0 collective-permute-done.before_ref
  24.2 0.0 collective-permute-done.1.after_ref
  24.2 3.6 %edges.1.mine_ref.image_ref = bf16[3,64,1024]{2,1,0:T(8,128)(2,1)S(1)} custom-call(s32[16,1024]{1,0:T(8,128)S(1)} %copy-done.4, bf16[3,3,16,1024]{3,2,1,0:T(8,128)(2,1)S(1)} %bitcast.9, bf16[3,64,256]{2,1,0:T(8,128)(2,1)S(1)} %collective-permute-done.before_ref, bf16[3,64,1024]{2,1,0:T(8,128)(2,1)S(1)} %copy-done.1, ...), custom_call_target="tpu_custom_call" | custom-call | flops 4000000000 | bytes 2000000 | tf_op jit(solution)/shard_map/edges/pallas_call | solution.py:163
  27.9 1.9 %collective-permute-start.2 = (bf16[3,64,1024]{2,1,0:T(8,128)(2,1)S(1)}, bf16[3,64,1024]{2,1,0:T(8,128)(2,1)S(1)}, u32[]{:S(2)}, u32[]{:S(2)}) collective-permute-start(bf16[3,64,1024]{2,1,0:T(8,128)(2,1)S(1)} %edges.1.mine_ref.image_ref), channel_id=1, source_target_pairs={{0,1},{1,0},{2,3},{3,2},{4,5},{5,4},{6,7},{7,6},{8,9},{9,8},{10,11... | collective-permute-start | bytes 1179656 | tf_op jit(solution)/shard_map/ppermute | solution.py:290
  29.8 0.0 copy-done.5
  29.8 0.0 copy-done.2
  29.8 0.9 %sampled.1.sampled_ref = f32[512,64]{1,0:T(8,128)S(1)} custom-call(s32[1,512]{1,0:T(1,128)S(1)} %bitcast.7, bf16[512,512]{1,0:T(8,128)(2,1)S(1)} %copy-done.2, bf16[3,64,1024]{2,1,0:T(8,128)(2,1)S(1)} %edges.1.mine_ref.image_ref), custom_call_target="tpu_custom_call" | custom-call | flops 2000000000 | bytes 2000000 | tf_op jit(solution)/shard_map/sampled/pallas_call | solution.py:196
  30.8 0.7 %collective-permute-done.2.theirs_ref = bf16[3,64,1024]{2,1,0:T(8,128)(2,1)S(1)} collective-permute-done((bf16[3,64,1024]{2,1,0:T(8,128)(2,1)S(1)}, bf16[3,64,1024]{2,1,0:T(8,128)(2,1)S(1)}, u32[]{:S(2)}, u32[]{:S(2)}) %collective-permute-start.2) | collective-permute-done | bytes 393248 | tf_op jit(solution)/shard_map/ppermute | solution.py:290
  31.5 0.0 all-to-all-done.basis_ref
  31.5 1.0 %reduced.1 = (f32[256,64]{1,0:T(8,128)S(1)}, f32[256,64]{1,0:T(8,128)S(1)}) custom-call(bf16[4,3,64,1024]{3,2,1,0:T(8,128)(2,1)S(1)} %all-to-all-done.basis_ref, bf16[3,64,1024]{2,1,0:T(8,128)(2,1)S(1)} %edges.1.mine_ref.image_ref, bf16[3,64,1024]{2,1,0:T(8,128)(2,1)S(1)} %collective-permute-done.2.theirs_ref), custom_call_target="tpu_custom_call" | custom-call | flops 2000000000 | bytes 2000000 | tf_op jit(solution)/shard_map/reduced/pallas_call | solution.py:220
  32.4 2.0 %all-gather = f32[512,64]{1,0:T(8,128)S(1)} all-gather(f32[256,64]{1,0:T(8,128)S(1)} %get-tuple-element.11), channel_id=2, replica_groups=mesh['y'=4,'z'=16,'x'=4,'core'=2] {'core'}, dimensions={0}, use_global_device_ids=true | all-gather | bytes 196608 | tf_op jit(solution)/shard_map/all_gather | solution.py:294
  34.4 0.1 joined.1
  34.5 31.0 %all_to_all.10.pieces_ref = bf16[64,8,128]{2,1,0:T(8,128)(2,1)S(1)} all-to-all(bf16[64,8,128]{2,1,0:T(8,128)(2,1)S(1)} %bitcast.6), channel_id=1, replica_groups=mesh['y'=4,'z'=16,'x'=4,'core'=2] {'y','z'}, dimensions={0} | all-to-all | bytes 262144 | tf_op jit(solution)/shard_map/all_to_all | solution.py:296
  65.5 0.7 %totals.1 = (f32[8,64]{1,0:T(8,128)}, f32[8,64]{1,0:T(8,128)}) custom-call(bf16[64,8,128]{2,1,0:T(8,128)(2,1)S(1)} %all_to_all.10.pieces_ref), custom_call_target="tpu_custom_call" | custom-call | tf_op jit(solution)/shard_map/totals/pallas_call | solution.py:264
  (1 shorter events, 0.0 us)
Async XLA Ops:
  0.6 1.0 %copy-start = (bf16[3,64,1024]{2,1,0:T(8,128)(2,1)S(1)}, bf16[3,64,1024]{2,1,0:T(8,128)(2,1)}, u32[]{:S(2)}) copy-start(bf16[3,64,1024]{2,1,0:T(8,128)(2,1)} %basis_ref.5) | copy-start | bytes 1179652
  2.9 17.6 %copy-start.1 = (bf16[3,64,1024]{2,1,0:T(8,128)(2,1)S(1)}, bf16[3,64,1024]{2,1,0:T(8,128)(2,1)}, u32[]{:S(2)}) copy-start(bf16[3,64,1024]{2,1,0:T(8,128)(2,1)} %basis_ref.5) | copy-start | bytes 1179652
  2.9 17.7 %copy-start.3 = (bf16[16,3,3,1024]{3,0,2,1:T(8,128)(2,1)S(1)}, bf16[16,3,3,1024]{3,0,2,1:T(8,128)(2,1)}, u32[]{:S(2)}) copy-start(bf16[16,3,3,1024]{3,0,2,1:T(8,128)(2,1)} %param.6) | copy-start | bytes 884740
  2.9 17.7 %copy-start.4 = (s32[16,1024]{1,0:T(8,128)S(1)}, s32[16,1024]{1,0:T(8,128)}, u32[]{:S(2)}) copy-start(s32[16,1024]{1,0:T(8,128)} %columns_ref.3) | copy-start | bytes 196612
  2.9 28.6 %all-to-all-start = ((bf16[4,3,64,1024]{3,2,1,0:T(8,128)(2,1)}), bf16[4,3,64,1024]{3,2,1,0:T(8,128)(2,1)S(1)}, u32[]{:S(2)}, u32[]{:S(2)}) async-start(bf16[4,3,64,1024]{3,2,1,0:T(8,128)(2,1)} %get-tuple-element.7), calls=%async_computation | async-start | bytes 3145728 | tf_op jit(solution)/shard_map/all_to_all | solution.py:280
  7.3 16.9 %collective-permute-start = (bf16[3,64,256]{2,1,0:T(8,128)(2,1)S(1)}, bf16[3,64,256]{2,1,0:T(8,128)(2,1)S(1)}, u32[]{:S(2)}, u32[]{:S(2)}) collective-permute-start(bf16[3,64,256]{2,1,0:T(8,128)(2,1)S(1)} %get-tuple-element.8), channel_id=1, source_target_pairs={{0,8},{8,16},{16,24},{24,32},{32,40},{40,48},{48,56},{56,64},{64,7... | collective-permute-start | bytes 294920 | tf_op jit(solution)/shard_map/ppermute | solution.py:281
  11.2 13.1 %collective-permute-start.1 = (bf16[3,64,256]{2,1,0:T(8,128)(2,1)S(1)}, bf16[3,64,256]{2,1,0:T(8,128)(2,1)S(1)}, u32[]{:S(2)}, u32[]{:S(2)}) collective-permute-start(bf16[3,64,256]{2,1,0:T(8,128)(2,1)S(1)} %get-tuple-element.9), channel_id=1, source_target_pairs={{8,0},{16,8},{24,16},{32,24},{40,32},{48,40},{56,48},{64,56},{72,6... | collective-permute-start | bytes 294920 | tf_op jit(solution)/shard_map/ppermute | solution.py:282
  24.2 5.6 %copy-start.5 = (s32[512]{0:T(512)S(1)}, s32[512]{0:T(512)}, u32[]{:S(2)}) copy-start(s32[512]{0:T(512)} %param.8) | copy-start | bytes 6148
  24.2 5.6 %copy-start.2 = (bf16[512,512]{1,0:T(8,128)(2,1)S(1)}, bf16[512,512]{1,0:T(8,128)(2,1)}, u32[]{:S(2)}) copy-start(bf16[512,512]{1,0:T(8,128)(2,1)} %inverse_ref.1) | copy-start | bytes 1572868
  27.9 3.6 %collective-permute-start.2 = (bf16[3,64,1024]{2,1,0:T(8,128)(2,1)S(1)}, bf16[3,64,1024]{2,1,0:T(8,128)(2,1)S(1)}, u32[]{:S(2)}, u32[]{:S(2)}) collective-permute-start(bf16[3,64,1024]{2,1,0:T(8,128)(2,1)S(1)} %edges.1.mine_ref.image_ref), channel_id=1, source_target_pairs={{0,1},{1,0},{2,3},{3,2},{4,5},{5,4},{6,7},{7,6},{8,9},{9,8},{10,11... | collective-permute-start | bytes 1179656 | tf_op jit(solution)/shard_map/ppermute | solution.py:290

commit v4 on v3

--- a/solution.py
+++ b/solution.py
@@ -105,30 +105,36 @@
     lax.fori_loop(0, (nodes - 2 * halo) // (2 * LANES), node_blocks, 0)
 
 
-def edge_kernel(
-    columns_ref, blocks_ref, before_ref, basis_ref, after_ref, inner_ref, image_ref, target_ref, weights_ref, extended_ref
-):
-    parts, modes, nodes = basis_ref.shape
-    halo = nodes // 4
-    window = LANES + 2 * halo
+def left_kernel(columns_ref, blocks_ref, before_ref, basis_ref, image_ref, target_ref, weights_ref, extended_ref):
+    parts, modes, halo = before_ref.shape
     for b in range(parts):
         rows = slice(b * modes, (b + 1) * modes)
-        extended_ref[0, rows, 0:halo] = before_ref[b]
-        extended_ref[0, rows, halo:] = basis_ref[b, :, : 2 * halo]
-        extended_ref[1, rows, : 2 * halo] = basis_ref[b, :, nodes - 2 * halo :]
-        extended_ref[1, rows, 2 * halo :] = after_ref[b]
+        extended_ref[rows, :halo] = before_ref[b]
+        extended_ref[rows, halo:] = basis_ref[b, :, : 2 * halo]
+    for k in range(halo // LANES):
+        here = slice(k * LANES, (k + 1) * LANES)
+        values = extended_ref[:, k * LANES : (k + 1) * LANES + 2 * halo]
+        scratch = (target_ref.at[k], weights_ref.at[k])
+        slot_sums(columns_ref, blocks_ref, *scratch, image_ref, values, here, here, halo)
+
+
+def right_kernel(
+    columns_ref, blocks_ref, after_ref, basis_ref, left_ref, inner_ref, image_ref, target_ref, weights_ref, extended_ref
+):
+    parts, modes, halo = after_ref.shape
+    nodes = basis_ref.shape[2]
+    for b in range(parts):
+        rows = slice(b * modes, (b + 1) * modes)
+        extended_ref[rows, : 2 * halo] = basis_ref[b, :, nodes - 2 * halo :]
+        extended_ref[rows, 2 * halo :] = after_ref[b]
+        image_ref[b, :, :halo] = left_ref[b]
         image_ref[b, :, halo : nodes - halo] = inner_ref[b]
-
-    def node_blocks(step, carry):
-        local = pl.multiple_of(step * LANES, LANES)
-        for side in range(2):
-            values = extended_ref[side, :, pl.ds(local, window)]
-            here = pl.ds(pl.multiple_of(local + side * (nodes - halo), LANES), LANES)
-            scratch = (target_ref.at[side], weights_ref.at[side])
-            slot_sums(columns_ref, blocks_ref, *scratch, image_ref, values, here, here, halo)
-        return carry
-
-    lax.fori_loop(0, halo // LANES, node_blocks, 0)
+    for k in range(halo // LANES):
+        first = nodes - halo + k * LANES
+        here = slice(first, first + LANES)
+        values = extended_ref[:, k * LANES : (k + 1) * LANES + 2 * halo]
+        scratch = (target_ref.at[k], weights_ref.at[k])
+        slot_sums(columns_ref, blocks_ref, *scratch, image_ref, values, here, here, halo)
 
 
 def slot_scratch(slots, parts):
@@ -157,19 +163,18 @@
     )(columns, blocks, in_vmem(basis))
 
 
-def edges(columns, blocks, before, basis, after, inner_image):
+def edge(kernel, columns, blocks, reached, basis, others, image_nodes):
     slots, _ = columns.shape
-    parts, modes, halo = before.shape
-    return pl.pallas_call(
-        edge_kernel,
-        out_shape=pltpu.VMEM(basis.shape, BF16),
+    parts, modes, halo = reached.shape
+    return pl.pallas_call(
+        kernel,
+        out_shape=pltpu.VMEM((parts, modes, image_nodes), BF16),
+        in_specs=[VMEM_SPEC] * (4 + len(others)),
         out_specs=VMEM_SPEC,
-        scratch_shapes=slot_scratch(slots, parts) + [pltpu.VMEM((2, parts * modes, 3 * halo), BF16)],
-        cost_estimate=cost(4 * 10**9, 2 * 10**6),
-        in_specs=[VMEM_SPEC] * 6,
-        compiler_params=PARAMS,
-        name="edges",
-    )(columns, blocks, in_vmem(before), in_vmem(basis), in_vmem(after), in_vmem(inner_image))
+        scratch_shapes=slot_scratch(slots, parts) + [pltpu.VMEM((parts * modes, 3 * halo), BF16)],
+        cost_estimate=cost(2 * 10**9, 10**6),
+        compiler_params=PARAMS,
+    )(columns, blocks, in_vmem(reached), in_vmem(basis), *(in_vmem(x) for x in others))
 
 
 def sampled_kernel(place_ref, inverse_ref, image_ref, out_ref):
@@ -206,12 +211,13 @@
 
 def reduced_kernel(basis_ref, mine_ref, theirs_ref, kept_ref, sent_ref):
     chips, parts, modes, nodes = basis_ref.shape
-    for image_ref, out_ref in ((mine_ref, kept_ref), (theirs_ref, sent_ref)):
-        total = jnp.zeros((chips * modes, modes), F32)
-        for c in range(parts):
-            rows = basis_ref[:, c].reshape(chips * modes, nodes)
-            total = total + lax.dot_general(rows, image_ref[c], (((1,), (1,)), ((), ())), preferred_element_type=F32)
-        out_ref[...] = total
+    total = jnp.zeros((chips * modes, 2 * modes), F32)
+    for c in range(parts):
+        rows = basis_ref[:, c].reshape(chips * modes, nodes)
+        both = jnp.concatenate([mine_ref[c], theirs_ref[c]], axis=0)
+        total = total + lax.dot_general(rows, both, (((1,), (1,)), ((), ())), preferred_element_type=F32)
+    kept_ref[...] = total[:, :modes]
+    sent_ref[...] = total[:, modes:]
 
 
 def reduced_rows(basis, mine, theirs):
@@ -282,7 +288,9 @@
     after = lax.ppermute(first, DOM, [((i + 1) % doms, i) for i in range(doms)])
     blocks = jnp.transpose(blocks, (1, 2, 0, 3))
     inner_image = inner(columns, blocks, mode_basis)
-    image = edges(columns, blocks, before, mode_basis, after, inner_image)
+    left_image = edge(left_kernel, columns, blocks, before, mode_basis, (), node_count // 4)
+    others = (left_image, inner_image)
+    image = edge(right_kernel, columns, blocks, after, mode_basis, others, node_count)
     node = samples // 3 - dom * node_count
     owned = (node >= 0) & (node < node_count)
     place = jnp.where(owned, (samples % 3) * node_count + node, -1)[None]

time: 66.6 us -> 66.3 us (level)
  waiting for transfers between devices: 0.71 us -> 3.76 us
  blocking collectives: 33 us -> 30 us
    ppermute x1, waiting for transfers between devices: 0.01 us -> 3.05 us  [shards(): before = lax.ppermute(last, DOM, [(i, (i + 1) % doms) for i in range(doms)])]
    all_to_all x1, blocking collectives: 31 us -> 28 us  [shards(): pieces = lax.all_to_all(partial.reshape(doms, -1, 2 * modes), DOM, 0, 0)]
    ppermute x1, starting transfers between devices: 3.81 us -> 1.92 us  [shards(): before = lax.ppermute(last, DOM, [(i, (i + 1) % doms) for i in range(doms)])]
    ppermute x1, starting transfers between devices: 9.38 us -> 11.3 us  [shards(): after = lax.ppermute(first, DOM, [((i + 1) % doms, i) for i in range(doms)])]
    pallas_call x1 -> x2, Pallas kernels: 3.61 us -> 3.56 us  [edge(): pl.pallas_call(kernel, out_shape=pltpu.VMEM((parts, modes, image_nodes),...]
  transfers between devices with their start and end apart: 4 -> 4, of which waited for: 1 -> 2; matrix products, arithmetic and copies ran while one was open for 0% -> 0% of each run, Pallas kernels for 12% -> 12%
where the time goes in v4:
time: 66.3 us; the launch traced here: 65.9 us
  blocking collectives  30 us (45%)
  starting transfers between devices  19.5 us (29%)
  Pallas kernels  10.8 us (16%)
  waiting for transfers between devices  3.76 us (6%)
  local copies, waits for them, and re-layouts  1.01 us (2%)
  between operations  0.78 us (1%)
    all_to_all x1, blocking collectives, shards(): pieces = lax.all_to_all(partial.reshape(doms, -1, 2 * modes), DOM, 0, 0)  28 us
    ppermute x1, starting transfers between devices, shards(): after = lax.ppermute(first, DOM, [((i + 1) % doms, i) for i in range(doms)])  11.3 us
    all_to_all x1, starting transfers between devices, shards(): mine = lax.all_to_all(copies, 'x', 0, 0)  4.42 us
    pallas_call x1, Pallas kernels, inner(): pl.pallas_call(inner_kernel, out_shape=pltpu.VMEM((parts, modes, nodes //...  3.59 us
    pallas_call x2, Pallas kernels, edge(): pl.pallas_call(kernel, out_shape=pltpu.VMEM((parts, modes, image_nodes),...  3.56 us
    ppermute x1, waiting for transfers between devices, shards(): before = lax.ppermute(last, DOM, [(i, (i + 1) % doms) for i in range(doms)])  3.05 us
    all_gather x1, blocking collectives, shards(): received = lax.all_gather(sent, 'core')  1.99 us
    ppermute x1, starting transfers between devices, shards(): other_image = lax.ppermute(image, 'core', pair)  1.92 us
  transfers between devices with their start and end apart: 4, of which 2 were waited for; matrix products, arithmetic and copies ran while one was open for 0% of the time, Pallas kernels for 12%

profile of v4, /device:TPU:8, one launch (start us, length us, event | category | flops | bytes accessed | tf_op | source)
XLA Modules:
  0.0 65.9 jit_solution(493227175475405634)
XLA Ops:
  0.6 0.0 copy-start
  0.6 1.0 %copy-done = bf16[3,64,1024]{2,1,0:T(8,128)(2,1)S(1)} copy-done((bf16[3,64,1024]{2,1,0:T(8,128)(2,1)S(1)}, bf16[3,64,1024]{2,1,0:T(8,128)(2,1)}, u32[]{:S(2)}) %copy-start) | copy-done | bytes 393240
  1.6 1.3 %spread.1 = (bf16[4,3,64,1024]{3,2,1,0:T(8,128)(2,1)}, bf16[3,64,256]{2,1,0:T(8,128)(2,1)S(1)}, bf16[3,64,256]{2,1,0:T(8,128)(2,1)S(1)}) custom-call(bf16[3,64,1024]{2,1,0:T(8,128)(2,1)S(1)} %copy-done), custom_call_target="tpu_custom_call" | custom-call | tf_op jit(solution)/shard_map/spread/pallas_call | solution.py:39
  2.9 0.0 copy-start.1
  2.9 0.0 copy-start.3
  2.9 0.0 copy-start.4
  2.9 4.4 %all-to-all-start = ((bf16[4,3,64,1024]{3,2,1,0:T(8,128)(2,1)}), bf16[4,3,64,1024]{3,2,1,0:T(8,128)(2,1)S(1)}, u32[]{:S(2)}, u32[]{:S(2)}) async-start(bf16[4,3,64,1024]{3,2,1,0:T(8,128)(2,1)} %get-tuple-element.7), calls=%async_computation | async-start | bytes 3145728 | tf_op jit(solution)/shard_map/all_to_all | solution.py:286
  7.3 11.3 %collective-permute-start = (bf16[3,64,256]{2,1,0:T(8,128)(2,1)S(1)}, bf16[3,64,256]{2,1,0:T(8,128)(2,1)S(1)}, u32[]{:S(2)}, u32[]{:S(2)}) collective-permute-start(bf16[3,64,256]{2,1,0:T(8,128)(2,1)S(1)} %get-tuple-element.8), channel_id=1, source_target_pairs={{8,0},{16,8},{24,16},{32,24},{40,32},{48,40},{56,48},{64,56},{72,6... | collective-permute-start | bytes 294920 | tf_op jit(solution)/shard_map/ppermute | solution.py:288
  18.6 1.9 %collective-permute-start.1 = (bf16[3,64,256]{2,1,0:T(8,128)(2,1)S(1)}, bf16[3,64,256]{2,1,0:T(8,128)(2,1)S(1)}, u32[]{:S(2)}, u32[]{:S(2)}) collective-permute-start(bf16[3,64,256]{2,1,0:T(8,128)(2,1)S(1)} %get-tuple-element.9), channel_id=1, source_target_pairs={{0,8},{8,16},{16,24},{24,32},{32,40},{40,48},{48,56},{56,64},{64,7... | collective-permute-start | bytes 294920 | tf_op jit(solution)/shard_map/ppermute | solution.py:287
  20.6 0.0 copy-done.1
  20.6 0.0 copy-done.3
  20.6 0.0 copy-done.4
  20.6 3.6 %inner.1.inner_ref = bf16[3,64,512]{2,1,0:T(8,128)(2,1)S(1)} custom-call(s32[16,1024]{1,0:T(8,128)S(1)} %copy-done.4, bf16[3,3,16,1024]{3,2,1,0:T(8,128)(2,1)S(1)} %bitcast.8, bf16[3,64,1024]{2,1,0:T(8,128)(2,1)S(1)} %copy-done.1), custom_call_target="tpu_custom_call" | custom-call | flops 4000000000 | bytes 2000000 | tf_op jit(solution)/shard_map/inner/pallas_call | solution.py:154
  24.2 3.1 %collective-permute-done.1.before_ref = bf16[3,64,256]{2,1,0:T(8,128)(2,1)S(1)} collective-permute-done((bf16[3,64,256]{2,1,0:T(8,128)(2,1)S(1)}, bf16[3,64,256]{2,1,0:T(8,128)(2,1)S(1)}, u32[]{:S(2)}, u32[]{:S(2)}) %collective-permute-start.1) | collective-permute-done | bytes 98336 | tf_op jit(solution)/shard_map/ppermute | solution.py:287
  27.2 1.8 %shard_map.68.left_ref = bf16[3,64,256]{2,1,0:T(8,128)(2,1)S(1)} custom-call(s32[16,1024]{1,0:T(8,128)S(1)} %copy-done.4, bf16[3,3,16,1024]{3,2,1,0:T(8,128)(2,1)S(1)} %bitcast.9, bf16[3,64,256]{2,1,0:T(8,128)(2,1)S(1)} %collective-permute-done.1.before_ref, bf16[3,64,1024]{2,1,0:T(8,128)(2,1)S(1)} %copy-done.1), custom_call_target="tpu_custom_call" | custom-call | flops 2000000000 | bytes 1000000 | tf_op jit(solution)/shard_map/pallas_call | solution.py:169
  29.0 0.0 copy-start.5
  29.0 0.0 copy-start.2
  29.1 0.0 collective-permute-done.after_ref
  29.1 1.8 %shard_map.69.mine_ref.image_ref = bf16[3,64,1024]{2,1,0:T(8,128)(2,1)S(1)} custom-call(s32[16,1024]{1,0:T(8,128)S(1)} %copy-done.4, bf16[3,3,16,1024]{3,2,1,0:T(8,128)(2,1)S(1)} %bitcast.10, bf16[3,64,256]{2,1,0:T(8,128)(2,1)S(1)} %collective-permute-done.after_ref, bf16[3,64,1024]{2,1,0:T(8,128)(2,1)S(1)} %copy-done.1, ...), custom_call_target="tpu_custom_call" | custom-call | flops 2000000000 | bytes 1000000 | tf_op jit(solution)/shard_map/pallas_call | solution.py:169
  30.9 1.9 %collective-permute-start.2 = (bf16[3,64,1024]{2,1,0:T(8,128)(2,1)S(1)}, bf16[3,64,1024]{2,1,0:T(8,128)(2,1)S(1)}, u32[]{:S(2)}, u32[]{:S(2)}) collective-permute-start(bf16[3,64,1024]{2,1,0:T(8,128)(2,1)S(1)} %shard_map.69.mine_ref.image_ref), channel_id=1, source_target_pairs={{0,1},{1,0},{2,3},{3,2},{4,5},{5,4},{6,7},{7,6},{8,9},{9,8},{10,11... | collective-permute-start | bytes 1179656 | tf_op jit(solution)/shard_map/ppermute | solution.py:298
  32.8 0.0 copy-done.5
  32.8 0.0 copy-done.2
  32.8 0.9 %sampled.1.sampled_ref = f32[512,64]{1,0:T(8,128)S(1)} custom-call(s32[1,512]{1,0:T(1,128)S(1)} %bitcast.7, bf16[512,512]{1,0:T(8,128)(2,1)S(1)} %copy-done.2, bf16[3,64,1024]{2,1,0:T(8,128)(2,1)S(1)} %shard_map.69.mine_ref.image_ref), custom_call_target="tpu_custom_call" | custom-call | flops 2000000000 | bytes 2000000 | tf_op jit(solution)/shard_map/sampled/pallas_call | solution.py:201
  33.8 0.7 %collective-permute-done.2.theirs_ref = bf16[3,64,1024]{2,1,0:T(8,128)(2,1)S(1)} collective-permute-done((bf16[3,64,1024]{2,1,0:T(8,128)(2,1)S(1)}, bf16[3,64,1024]{2,1,0:T(8,128)(2,1)S(1)}, u32[]{:S(2)}, u32[]{:S(2)}) %collective-permute-start.2) | collective-permute-done | bytes 393248 | tf_op jit(solution)/shard_map/ppermute | solution.py:298
  34.5 0.0 all-to-all-done.basis_ref
  34.5 0.6 reduced.1
  35.1 2.0 %all-gather = f32[512,64]{1,0:T(8,128)S(1)} all-gather(f32[256,64]{1,0:T(8,128)S(1)} %get-tuple-element.11), channel_id=2, replica_groups=mesh['y'=4,'z'=16,'x'=4,'core'=2] {'core'}, dimensions={0}, use_global_device_ids=true | all-gather | bytes 196608 | tf_op jit(solution)/shard_map/all_gather | solution.py:302
  37.1 0.1 joined.1
  37.2 28.0 %all_to_all.10.pieces_ref = bf16[64,8,128]{2,1,0:T(8,128)(2,1)S(1)} all-to-all(bf16[64,8,128]{2,1,0:T(8,128)(2,1)S(1)} %bitcast.6), channel_id=1, replica_groups=mesh['y'=4,'z'=16,'x'=4,'core'=2] {'y','z'}, dimensions={0} | all-to-all | bytes 262144 | tf_op jit(solution)/shard_map/all_to_all | solution.py:304
  65.2 0.7 %totals.1 = (f32[8,64]{1,0:T(8,128)}, f32[8,64]{1,0:T(8,128)}) custom-call(bf16[64,8,128]{2,1,0:T(8,128)(2,1)S(1)} %all_to_all.10.pieces_ref), custom_call_target="tpu_custom_call" | custom-call | tf_op jit(solution)/shard_map/totals/pallas_call | solution.py:270
  (1 shorter events, 0.0 us)
Async XLA Ops:
  0.6 1.0 %copy-start = (bf16[3,64,1024]{2,1,0:T(8,128)(2,1)S(1)}, bf16[3,64,1024]{2,1,0:T(8,128)(2,1)}, u32[]{:S(2)}) copy-start(bf16[3,64,1024]{2,1,0:T(8,128)(2,1)} %basis_ref.7) | copy-start | bytes 1179652
  2.9 17.6 %copy-start.1 = (bf16[3,64,1024]{2,1,0:T(8,128)(2,1)S(1)}, bf16[3,64,1024]{2,1,0:T(8,128)(2,1)}, u32[]{:S(2)}) copy-start(bf16[3,64,1024]{2,1,0:T(8,128)(2,1)} %basis_ref.7) | copy-start | bytes 1179652
  2.9 17.7 %copy-start.3 = (bf16[16,3,3,1024]{3,0,2,1:T(8,128)(2,1)S(1)}, bf16[16,3,3,1024]{3,0,2,1:T(8,128)(2,1)}, u32[]{:S(2)}) copy-start(bf16[16,3,3,1024]{3,0,2,1:T(8,128)(2,1)} %param.6) | copy-start | bytes 884740
  2.9 17.7 %copy-start.4 = (s32[16,1024]{1,0:T(8,128)S(1)}, s32[16,1024]{1,0:T(8,128)}, u32[]{:S(2)}) copy-start(s32[16,1024]{1,0:T(8,128)} %columns_ref.5) | copy-start | bytes 196612
  2.9 31.6 %all-to-all-start = ((bf16[4,3,64,1024]{3,2,1,0:T(8,128)(2,1)}), bf16[4,3,64,1024]{3,2,1,0:T(8,128)(2,1)S(1)}, u32[]{:S(2)}, u32[]{:S(2)}) async-start(bf16[4,3,64,1024]{3,2,1,0:T(8,128)(2,1)} %get-tuple-element.7), calls=%async_computation | async-start | bytes 3145728 | tf_op jit(solution)/shard_map/all_to_all | solution.py:286
  7.3 21.7 %collective-permute-start = (bf16[3,64,256]{2,1,0:T(8,128)(2,1)S(1)}, bf16[3,64,256]{2,1,0:T(8,128)(2,1)S(1)}, u32[]{:S(2)}, u32[]{:S(2)}) collective-permute-start(bf16[3,64,256]{2,1,0:T(8,128)(2,1)S(1)} %get-tuple-element.8), channel_id=1, source_target_pairs={{8,0},{16,8},{24,16},{32,24},{40,32},{48,40},{56,48},{64,56},{72,6... | collective-permute-start | bytes 294920 | tf_op jit(solution)/shard_map/ppermute | solution.py:288
  18.6 8.6 %collective-permute-start.1 = (bf16[3,64,256]{2,1,0:T(8,128)(2,1)S(1)}, bf16[3,64,256]{2,1,0:T(8,128)(2,1)S(1)}, u32[]{:S(2)}, u32[]{:S(2)}) collective-permute-start(bf16[3,64,256]{2,1,0:T(8,128)(2,1)S(1)} %get-tuple-element.9), channel_id=1, source_target_pairs={{0,8},{8,16},{16,24},{24,32},{32,40},{40,48},{48,56},{56,64},{64,7... | collective-permute-start | bytes 294920 | tf_op jit(solution)/shard_map/ppermute | solution.py:287
  29.0 3.8 %copy-start.5 = (s32[512]{0:T(512)S(1)}, s32[512]{0:T(512)}, u32[]{:S(2)}) copy-start(s32[512]{0:T(512)} %param.8) | copy-start | bytes 6148
  29.0 3.8 %copy-start.2 = (bf16[512,512]{1,0:T(8,128)(2,1)S(1)}, bf16[512,512]{1,0:T(8,128)(2,1)}, u32[]{:S(2)}) copy-start(bf16[512,512]{1,0:T(8,128)(2,1)} %inverse_ref.1) | copy-start | bytes 1572868
  30.9 3.6 %collective-permute-start.2 = (bf16[3,64,1024]{2,1,0:T(8,128)(2,1)S(1)}, bf16[3,64,1024]{2,1,0:T(8,128)(2,1)S(1)}, u32[]{:S(2)}, u32[]{:S(2)}) collective-permute-start(bf16[3,64,1024]{2,1,0:T(8,128)(2,1)S(1)} %shard_map.69.mine_ref.image_ref), channel_id=1, source_target_pairs={{0,1},{1,0},{2,3},{3,2},{4,5},{5,4},{6,7},{7,6},{8,9},{9,8},{10,11... | collective-permute-start | bytes 1179656 | tf_op jit(solution)/shard_map/ppermute | solution.py:298

commit v5 on v4

--- a/solution.py
+++ b/solution.py
@@ -25,12 +25,15 @@
 VMEM_SPEC = pl.BlockSpec(memory_space=pltpu.VMEM)
 
 
-def spread_kernel(basis_ref, copies_ref, first_ref, last_ref):
+def spread_kernel(basis_ref, copies_ref, first_ref, last_ref, sems):
     nodes, halo = basis_ref.shape[2], first_ref.shape[2]
-    for x in range(copies_ref.shape[0]):
-        copies_ref[x] = basis_ref[...]
+    moves = [pltpu.make_async_copy(basis_ref, copies_ref.at[x], sems.at[x]) for x in range(copies_ref.shape[0])]
+    for move in moves:
+        move.start()
     first_ref[...] = basis_ref[:, :, :halo]
     last_ref[...] = basis_ref[:, :, nodes - halo :]
+    for move in moves:
+        move.wait()
 
 
 def spread(basis, chips):
@@ -38,12 +41,13 @@
     side = pltpu.VMEM((parts, modes, nodes // 4), BF16)
     return pl.pallas_call(
         spread_kernel,
-        out_shape=(pltpu.VMEM((chips, *basis.shape), BF16), side, side),
+        out_shape=(jax.ShapeDtypeStruct((chips, *basis.shape), BF16), side, side),
         in_specs=[VMEM_SPEC],
-        out_specs=(VMEM_SPEC,) * 3,
+        out_specs=(pl.BlockSpec(memory_space=pltpu.HBM), VMEM_SPEC, VMEM_SPEC),
+        scratch_shapes=[pltpu.SemaphoreType.DMA((chips,))],
         compiler_params=PARAMS,
         name="spread",
-    )(basis)
+    )(in_vmem(basis))
 
 
 def slot_sums(columns_ref, blocks_ref, target_ref, weights_ref, image_ref, values, here, there, halo):

time: 66.3 us -> 66.2 us (level)
  no operation moved by 1% of the time
where the time goes in v5:
time: 66.2 us; the launch traced here: 65.9 us
  blocking collectives  30 us (45%)
  starting transfers between devices  19.6 us (30%)
  Pallas kernels  10.7 us (16%)
  waiting for transfers between devices  3.77 us (6%)
  local copies, waits for them, and re-layouts  1.02 us (2%)
  between operations  0.81 us (1%)
    all_to_all x1, blocking collectives, shards(): pieces = lax.all_to_all(partial.reshape(doms, -1, 2 * modes), DOM, 0, 0)  28 us
    ppermute x1, starting transfers between devices, shards(): after = lax.ppermute(first, DOM, [((i + 1) % doms, i) for i in range(doms)])  11.3 us
    all_to_all x1, starting transfers between devices, shards(): mine = lax.all_to_all(copies, 'x', 0, 0)  4.44 us
    pallas_call x1, Pallas kernels, inner(): pl.pallas_call(inner_kernel, out_shape=pltpu.VMEM((parts, modes, nodes //...  3.58 us
    pallas_call x2, Pallas kernels, edge(): pl.pallas_call(kernel, out_shape=pltpu.VMEM((parts, modes, image_nodes),...  3.56 us
    ppermute x1, waiting for transfers between devices, shards(): before = lax.ppermute(last, DOM, [(i, (i + 1) % doms) for i in range(doms)])  3.06 us
    all_gather x1, blocking collectives, shards(): received = lax.all_gather(sent, 'core')  1.99 us
    ppermute x1, starting transfers between devices, shards(): before = lax.ppermute(last, DOM, [(i, (i + 1) % doms) for i in range(doms)])  1.92 us
  transfers between devices with their start and end apart: 4, of which 2 were waited for; matrix products, arithmetic and copies ran while one was open for 0% of the time, Pallas kernels for 12%

profile of v5, /device:TPU:8, one launch (start us, length us, event | category | flops | bytes accessed | tf_op | source)
XLA Modules:
  0.0 65.9 jit_solution(7475548637755852328)
XLA Ops:
  0.6 0.0 copy-start
  0.6 1.0 %copy-done = bf16[3,64,1024]{2,1,0:T(8,128)(2,1)S(1)} copy-done((bf16[3,64,1024]{2,1,0:T(8,128)(2,1)S(1)}, bf16[3,64,1024]{2,1,0:T(8,128)(2,1)}, u32[]{:S(2)}) %copy-start) | copy-done | bytes 393240
  1.6 1.2 %spread.1 = (bf16[4,3,64,1024]{3,2,1,0:T(8,128)(2,1)}, bf16[3,64,256]{2,1,0:T(8,128)(2,1)S(1)}, bf16[3,64,256]{2,1,0:T(8,128)(2,1)S(1)}) custom-call(bf16[3,64,1024]{2,1,0:T(8,128)(2,1)S(1)} %copy-done), custom_call_target="tpu_custom_call" | custom-call | tf_op jit(solution)/shard_map/spread/pallas_call | solution.py:42
  2.8 0.0 copy-start.1
  2.9 0.0 copy-start.3
  2.9 0.0 copy-start.4
  2.9 4.4 %all-to-all-start = ((bf16[4,3,64,1024]{3,2,1,0:T(8,128)(2,1)}), bf16[4,3,64,1024]{3,2,1,0:T(8,128)(2,1)S(1)}, u32[]{:S(2)}, u32[]{:S(2)}) async-start(bf16[4,3,64,1024]{3,2,1,0:T(8,128)(2,1)} %get-tuple-element.7), calls=%async_computation | async-start | bytes 3145728 | tf_op jit(solution)/shard_map/all_to_all | solution.py:290
  7.3 11.3 %collective-permute-start = (bf16[3,64,256]{2,1,0:T(8,128)(2,1)S(1)}, bf16[3,64,256]{2,1,0:T(8,128)(2,1)S(1)}, u32[]{:S(2)}, u32[]{:S(2)}) collective-permute-start(bf16[3,64,256]{2,1,0:T(8,128)(2,1)S(1)} %get-tuple-element.8), channel_id=1, source_target_pairs={{8,0},{16,8},{24,16},{32,24},{40,32},{48,40},{56,48},{64,56},{72,6... | collective-permute-start | bytes 294920 | tf_op jit(solution)/shard_map/ppermute | solution.py:292
  18.6 1.9 %collective-permute-start.1 = (bf16[3,64,256]{2,1,0:T(8,128)(2,1)S(1)}, bf16[3,64,256]{2,1,0:T(8,128)(2,1)S(1)}, u32[]{:S(2)}, u32[]{:S(2)}) collective-permute-start(bf16[3,64,256]{2,1,0:T(8,128)(2,1)S(1)} %get-tuple-element.9), channel_id=1, source_target_pairs={{0,8},{8,16},{16,24},{24,32},{32,40},{40,48},{48,56},{56,64},{64,7... | collective-permute-start | bytes 294920 | tf_op jit(solution)/shard_map/ppermute | solution.py:291
  20.5 0.0 copy-done.1
  20.5 0.0 copy-done.3
  20.5 0.0 copy-done.4
  20.6 3.6 %inner.1.inner_ref = bf16[3,64,512]{2,1,0:T(8,128)(2,1)S(1)} custom-call(s32[16,1024]{1,0:T(8,128)S(1)} %copy-done.4, bf16[3,3,16,1024]{3,2,1,0:T(8,128)(2,1)S(1)} %bitcast.8, bf16[3,64,1024]{2,1,0:T(8,128)(2,1)S(1)} %copy-done.1), custom_call_target="tpu_custom_call" | custom-call | flops 4000000000 | bytes 2000000 | tf_op jit(solution)/shard_map/inner/pallas_call | solution.py:158
  24.2 3.1 %collective-permute-done.1.before_ref = bf16[3,64,256]{2,1,0:T(8,128)(2,1)S(1)} collective-permute-done((bf16[3,64,256]{2,1,0:T(8,128)(2,1)S(1)}, bf16[3,64,256]{2,1,0:T(8,128)(2,1)S(1)}, u32[]{:S(2)}, u32[]{:S(2)}) %collective-permute-start.1) | collective-permute-done | bytes 98336 | tf_op jit(solution)/shard_map/ppermute | solution.py:291
  27.2 1.8 %shard_map.68.left_ref = bf16[3,64,256]{2,1,0:T(8,128)(2,1)S(1)} custom-call(s32[16,1024]{1,0:T(8,128)S(1)} %copy-done.4, bf16[3,3,16,1024]{3,2,1,0:T(8,128)(2,1)S(1)} %bitcast.9, bf16[3,64,256]{2,1,0:T(8,128)(2,1)S(1)} %collective-permute-done.1.before_ref, bf16[3,64,1024]{2,1,0:T(8,128)(2,1)S(1)} %copy-done.1), custom_call_target="tpu_custom_call" | custom-call | flops 2000000000 | bytes 1000000 | tf_op jit(solution)/shard_map/pallas_call | solution.py:173
  29.0 0.0 copy-start.5
  29.0 0.0 copy-start.2
  29.0 0.0 collective-permute-done.after_ref
  29.0 1.8 %shard_map.69.mine_ref.image_ref = bf16[3,64,1024]{2,1,0:T(8,128)(2,1)S(1)} custom-call(s32[16,1024]{1,0:T(8,128)S(1)} %copy-done.4, bf16[3,3,16,1024]{3,2,1,0:T(8,128)(2,1)S(1)} %bitcast.10, bf16[3,64,256]{2,1,0:T(8,128)(2,1)S(1)} %collective-permute-done.after_ref, bf16[3,64,1024]{2,1,0:T(8,128)(2,1)S(1)} %copy-done.1, ...), custom_call_target="tpu_custom_call" | custom-call | flops 2000000000 | bytes 1000000 | tf_op jit(solution)/shard_map/pallas_call | solution.py:173
  30.8 1.9 %collective-permute-start.2 = (bf16[3,64,1024]{2,1,0:T(8,128)(2,1)S(1)}, bf16[3,64,1024]{2,1,0:T(8,128)(2,1)S(1)}, u32[]{:S(2)}, u32[]{:S(2)}) collective-permute-start(bf16[3,64,1024]{2,1,0:T(8,128)(2,1)S(1)} %shard_map.69.mine_ref.image_ref), channel_id=1, source_target_pairs={{0,1},{1,0},{2,3},{3,2},{4,5},{5,4},{6,7},{7,6},{8,9},{9,8},{10,11... | collective-permute-start | bytes 1179656 | tf_op jit(solution)/shard_map/ppermute | solution.py:302
  32.8 0.0 copy-done.5
  32.8 0.0 copy-done.2
  32.8 0.9 %sampled.1.sampled_ref = f32[512,64]{1,0:T(8,128)S(1)} custom-call(s32[1,512]{1,0:T(1,128)S(1)} %bitcast.7, bf16[512,512]{1,0:T(8,128)(2,1)S(1)} %copy-done.2, bf16[3,64,1024]{2,1,0:T(8,128)(2,1)S(1)} %shard_map.69.mine_ref.image_ref), custom_call_target="tpu_custom_call" | custom-call | flops 2000000000 | bytes 2000000 | tf_op jit(solution)/shard_map/sampled/pallas_call | solution.py:205
  33.7 0.7 %collective-permute-done.2.theirs_ref = bf16[3,64,1024]{2,1,0:T(8,128)(2,1)S(1)} collective-permute-done((bf16[3,64,1024]{2,1,0:T(8,128)(2,1)S(1)}, bf16[3,64,1024]{2,1,0:T(8,128)(2,1)S(1)}, u32[]{:S(2)}, u32[]{:S(2)}) %collective-permute-start.2) | collective-permute-done | bytes 393248 | tf_op jit(solution)/shard_map/ppermute | solution.py:302
  34.4 0.0 all-to-all-done.basis_ref
  34.4 0.6 reduced.1
  35.1 2.0 %all-gather = f32[512,64]{1,0:T(8,128)S(1)} all-gather(f32[256,64]{1,0:T(8,128)S(1)} %get-tuple-element.11), channel_id=2, replica_groups=mesh['y'=4,'z'=16,'x'=4,'core'=2] {'core'}, dimensions={0}, use_global_device_ids=true | all-gather | bytes 196608 | tf_op jit(solution)/shard_map/all_gather | solution.py:306
  37.1 0.1 joined.1
  37.2 28.0 %all_to_all.10.pieces_ref = bf16[64,8,128]{2,1,0:T(8,128)(2,1)S(1)} all-to-all(bf16[64,8,128]{2,1,0:T(8,128)(2,1)S(1)} %bitcast.6), channel_id=1, replica_groups=mesh['y'=4,'z'=16,'x'=4,'core'=2] {'y','z'}, dimensions={0} | all-to-all | bytes 262144 | tf_op jit(solution)/shard_map/all_to_all | solution.py:308
  65.2 0.7 %totals.1 = (f32[8,64]{1,0:T(8,128)}, f32[8,64]{1,0:T(8,128)}) custom-call(bf16[64,8,128]{2,1,0:T(8,128)(2,1)S(1)} %all_to_all.10.pieces_ref), custom_call_target="tpu_custom_call" | custom-call | tf_op jit(solution)/shard_map/totals/pallas_call | solution.py:274
  (1 shorter events, 0.0 us)
Async XLA Ops:
  0.6 1.0 %copy-start = (bf16[3,64,1024]{2,1,0:T(8,128)(2,1)S(1)}, bf16[3,64,1024]{2,1,0:T(8,128)(2,1)}, u32[]{:S(2)}) copy-start(bf16[3,64,1024]{2,1,0:T(8,128)(2,1)} %basis_ref.7) | copy-start | bytes 1179652
  2.8 17.7 %copy-start.1 = (bf16[3,64,1024]{2,1,0:T(8,128)(2,1)S(1)}, bf16[3,64,1024]{2,1,0:T(8,128)(2,1)}, u32[]{:S(2)}) copy-start(bf16[3,64,1024]{2,1,0:T(8,128)(2,1)} %basis_ref.7) | copy-start | bytes 1179652
  2.9 17.7 %copy-start.3 = (bf16[16,3,3,1024]{3,0,2,1:T(8,128)(2,1)S(1)}, bf16[16,3,3,1024]{3,0,2,1:T(8,128)(2,1)}, u32[]{:S(2)}) copy-start(bf16[16,3,3,1024]{3,0,2,1:T(8,128)(2,1)} %param.6) | copy-start | bytes 884740
  2.9 17.7 %copy-start.4 = (s32[16,1024]{1,0:T(8,128)S(1)}, s32[16,1024]{1,0:T(8,128)}, u32[]{:S(2)}) copy-start(s32[16,1024]{1,0:T(8,128)} %columns_ref.5) | copy-start | bytes 196612
  2.9 31.6 %all-to-all-start = ((bf16[4,3,64,1024]{3,2,1,0:T(8,128)(2,1)}), bf16[4,3,64,1024]{3,2,1,0:T(8,128)(2,1)S(1)}, u32[]{:S(2)}, u32[]{:S(2)}) async-start(bf16[4,3,64,1024]{3,2,1,0:T(8,128)(2,1)} %get-tuple-element.7), calls=%async_computation | async-start | bytes 3145728 | tf_op jit(solution)/shard_map/all_to_all | solution.py:290
  7.3 21.7 %collective-permute-start = (bf16[3,64,256]{2,1,0:T(8,128)(2,1)S(1)}, bf16[3,64,256]{2,1,0:T(8,128)(2,1)S(1)}, u32[]{:S(2)}, u32[]{:S(2)}) collective-permute-start(bf16[3,64,256]{2,1,0:T(8,128)(2,1)S(1)} %get-tuple-element.8), channel_id=1, source_target_pairs={{8,0},{16,8},{24,16},{32,24},{40,32},{48,40},{56,48},{64,56},{72,6... | collective-permute-start | bytes 294920 | tf_op jit(solution)/shard_map/ppermute | solution.py:292
  18.6 8.6 %collective-permute-start.1 = (bf16[3,64,256]{2,1,0:T(8,128)(2,1)S(1)}, bf16[3,64,256]{2,1,0:T(8,128)(2,1)S(1)}, u32[]{:S(2)}, u32[]{:S(2)}) collective-permute-start(bf16[3,64,256]{2,1,0:T(8,128)(2,1)S(1)} %get-tuple-element.9), channel_id=1, source_target_pairs={{0,8},{8,16},{16,24},{24,32},{32,40},{40,48},{48,56},{56,64},{64,7... | collective-permute-start | bytes 294920 | tf_op jit(solution)/shard_map/ppermute | solution.py:291
  29.0 3.8 %copy-start.5 = (s32[512]{0:T(512)S(1)}, s32[512]{0:T(512)}, u32[]{:S(2)}) copy-start(s32[512]{0:T(512)} %param.8) | copy-start | bytes 6148
  29.0 3.8 %copy-start.2 = (bf16[512,512]{1,0:T(8,128)(2,1)S(1)}, bf16[512,512]{1,0:T(8,128)(2,1)}, u32[]{:S(2)}) copy-start(bf16[512,512]{1,0:T(8,128)(2,1)} %inverse_ref.1) | copy-start | bytes 1572868
  30.8 3.6 %collective-permute-start.2 = (bf16[3,64,1024]{2,1,0:T(8,128)(2,1)S(1)}, bf16[3,64,1024]{2,1,0:T(8,128)(2,1)S(1)}, u32[]{:S(2)}, u32[]{:S(2)}) collective-permute-start(bf16[3,64,1024]{2,1,0:T(8,128)(2,1)S(1)} %shard_map.69.mine_ref.image_ref), channel_id=1, source_target_pairs={{0,1},{1,0},{2,3},{3,2},{4,5},{5,4},{6,7},{7,6},{8,9},{9,8},{10,11... | collective-permute-start | bytes 1179656 | tf_op jit(solution)/shard_map/ppermute | solution.py:302

commit v6 on v5

--- a/solution.py
+++ b/solution.py
@@ -221,16 +221,18 @@
         both = jnp.concatenate([mine_ref[c], theirs_ref[c]], axis=0)
         total = total + lax.dot_general(rows, both, (((1,), (1,)), ((), ())), preferred_element_type=F32)
     kept_ref[...] = total[:, :modes]
-    sent_ref[...] = total[:, modes:]
+    half = chips * modes // 2
+    sent_ref[...] = jnp.concatenate([total[:half, modes:], total[half:, modes:]], axis=1)
 
 
 def reduced_rows(basis, mine, theirs):
     chips, _, modes, _ = basis.shape
-    out = pltpu.VMEM((chips * modes, modes), F32)
+    kept = pltpu.VMEM((chips * modes, modes), F32)
+    sent = pltpu.VMEM((chips * modes // 2, 2 * modes), F32)
     return pl.pallas_call(
         reduced_kernel,
         in_specs=[VMEM_SPEC] * 3,
-        out_shape=(out, out),
+        out_shape=(kept, sent),
         out_specs=(VMEM_SPEC, VMEM_SPEC),
         cost_estimate=cost(2 * 10**9, 2 * 10**6),
         compiler_params=PARAMS,
@@ -241,9 +243,12 @@
 def joined_kernel(core_ref, kept_ref, received_ref, sampled_ref, out_ref):
     modes = kept_ref.shape[1]
     core = core_ref[0]
-    for x in range(kept_ref.shape[0] // modes):
+    chips = kept_ref.shape[0] // modes
+    for x in range(chips):
         rows = slice(x * modes, (x + 1) * modes)
-        for source, left in ((core, kept_ref[rows, :]), (1 - core, received_ref[1 - core, rows, :])):
+        side, row = divmod(x, chips // 2)
+        packed = (slice(row * modes, (row + 1) * modes), slice(side * modes, (side + 1) * modes))
+        for source, left in ((core, kept_ref[rows, :]), (1 - core, received_ref[(1 - core, *packed)])):
             first = pl.multiple_of((2 * x + source) * modes, modes)
             right = sampled_ref[pl.ds(first, modes), :]
             out_ref[pl.ds(first, modes), :] = jnp.concatenate([left, right], axis=1).astype(out_ref.dtype)

time: 66.2 us -> 66.1 us (level)
  no operation moved by 1% of the time
where the time goes in v6:
time: 66.1 us; the launch traced here: 65.8 us
  blocking collectives  29.9 us (45%)
  starting transfers between devices  19.6 us (30%)
  Pallas kernels  10.7 us (16%)
  waiting for transfers between devices  3.77 us (6%)
  local copies, waits for them, and re-layouts  1.02 us (2%)
  between operations  0.82 us (1%)
    all_to_all x1, blocking collectives, shards(): pieces = lax.all_to_all(partial.reshape(doms, -1, 2 * modes), DOM, 0, 0)  28 us
    ppermute x1, starting transfers between devices, shards(): after = lax.ppermute(first, DOM, [((i + 1) % doms, i) for i in range(doms)])  11.3 us
    all_to_all x1, starting transfers between devices, shards(): mine = lax.all_to_all(copies, 'x', 0, 0)  4.44 us
    pallas_call x1, Pallas kernels, inner(): pl.pallas_call(inner_kernel, out_shape=pltpu.VMEM((parts, modes, nodes //...  3.58 us
    pallas_call x2, Pallas kernels, edge(): pl.pallas_call(kernel, out_shape=pltpu.VMEM((parts, modes, image_nodes),...  3.56 us
    ppermute x1, waiting for transfers between devices, shards(): before = lax.ppermute(last, DOM, [(i, (i + 1) % doms) for i in range(doms)])  3.06 us
    ppermute x1, starting transfers between devices, shards(): before = lax.ppermute(last, DOM, [(i, (i + 1) % doms) for i in range(doms)])  1.92 us
    ppermute x1, starting transfers between devices, shards(): other_image = lax.ppermute(image, 'core', pair)  1.92 us
  transfers between devices with their start and end apart: 4, of which 2 were waited for; matrix products, arithmetic and copies ran while one was open for 0% of the time, Pallas kernels for 12%

profile of v6, /device:TPU:8, one launch (start us, length us, event | category | flops | bytes accessed | tf_op | source)
XLA Modules:
  0.0 65.8 jit_solution(10279020441863034683)
XLA Ops:
  0.6 0.0 copy-start
  0.6 1.0 %copy-done = bf16[3,64,1024]{2,1,0:T(8,128)(2,1)S(1)} copy-done((bf16[3,64,1024]{2,1,0:T(8,128)(2,1)S(1)}, bf16[3,64,1024]{2,1,0:T(8,128)(2,1)}, u32[]{:S(2)}) %copy-start) | copy-done | bytes 393240
  1.6 1.2 %spread.1 = (bf16[4,3,64,1024]{3,2,1,0:T(8,128)(2,1)}, bf16[3,64,256]{2,1,0:T(8,128)(2,1)S(1)}, bf16[3,64,256]{2,1,0:T(8,128)(2,1)S(1)}) custom-call(bf16[3,64,1024]{2,1,0:T(8,128)(2,1)S(1)} %copy-done), custom_call_target="tpu_custom_call" | custom-call | tf_op jit(solution)/shard_map/spread/pallas_call | solution.py:42
  2.8 0.0 copy-start.1
  2.9 0.0 copy-start.3
  2.9 0.0 copy-start.4
  2.9 4.4 %all-to-all-start = ((bf16[4,3,64,1024]{3,2,1,0:T(8,128)(2,1)}), bf16[4,3,64,1024]{3,2,1,0:T(8,128)(2,1)S(1)}, u32[]{:S(2)}, u32[]{:S(2)}) async-start(bf16[4,3,64,1024]{3,2,1,0:T(8,128)(2,1)} %get-tuple-element.7), calls=%async_computation | async-start | bytes 3145728 | tf_op jit(solution)/shard_map/all_to_all | solution.py:295
  7.3 11.3 %collective-permute-start = (bf16[3,64,256]{2,1,0:T(8,128)(2,1)S(1)}, bf16[3,64,256]{2,1,0:T(8,128)(2,1)S(1)}, u32[]{:S(2)}, u32[]{:S(2)}) collective-permute-start(bf16[3,64,256]{2,1,0:T(8,128)(2,1)S(1)} %get-tuple-element.8), channel_id=1, source_target_pairs={{8,0},{16,8},{24,16},{32,24},{40,32},{48,40},{56,48},{64,56},{72,6... | collective-permute-start | bytes 294920 | tf_op jit(solution)/shard_map/ppermute | solution.py:297
  18.6 1.9 %collective-permute-start.1 = (bf16[3,64,256]{2,1,0:T(8,128)(2,1)S(1)}, bf16[3,64,256]{2,1,0:T(8,128)(2,1)S(1)}, u32[]{:S(2)}, u32[]{:S(2)}) collective-permute-start(bf16[3,64,256]{2,1,0:T(8,128)(2,1)S(1)} %get-tuple-element.9), channel_id=1, source_target_pairs={{0,8},{8,16},{16,24},{24,32},{32,40},{40,48},{48,56},{56,64},{64,7... | collective-permute-start | bytes 294920 | tf_op jit(solution)/shard_map/ppermute | solution.py:296
  20.5 0.0 copy-done.1
  20.5 0.0 copy-done.3
  20.5 0.0 copy-done.4
  20.6 3.6 %inner.1.inner_ref = bf16[3,64,512]{2,1,0:T(8,128)(2,1)S(1)} custom-call(s32[16,1024]{1,0:T(8,128)S(1)} %copy-done.4, bf16[3,3,16,1024]{3,2,1,0:T(8,128)(2,1)S(1)} %bitcast.8, bf16[3,64,1024]{2,1,0:T(8,128)(2,1)S(1)} %copy-done.1), custom_call_target="tpu_custom_call" | custom-call | flops 4000000000 | bytes 2000000 | tf_op jit(solution)/shard_map/inner/pallas_call | solution.py:158
  24.2 3.1 %collective-permute-done.1.before_ref = bf16[3,64,256]{2,1,0:T(8,128)(2,1)S(1)} collective-permute-done((bf16[3,64,256]{2,1,0:T(8,128)(2,1)S(1)}, bf16[3,64,256]{2,1,0:T(8,128)(2,1)S(1)}, u32[]{:S(2)}, u32[]{:S(2)}) %collective-permute-start.1) | collective-permute-done | bytes 98336 | tf_op jit(solution)/shard_map/ppermute | solution.py:296
  27.2 1.8 %shard_map.68.left_ref = bf16[3,64,256]{2,1,0:T(8,128)(2,1)S(1)} custom-call(s32[16,1024]{1,0:T(8,128)S(1)} %copy-done.4, bf16[3,3,16,1024]{3,2,1,0:T(8,128)(2,1)S(1)} %bitcast.9, bf16[3,64,256]{2,1,0:T(8,128)(2,1)S(1)} %collective-permute-done.1.before_ref, bf16[3,64,1024]{2,1,0:T(8,128)(2,1)S(1)} %copy-done.1), custom_call_target="tpu_custom_call" | custom-call | flops 2000000000 | bytes 1000000 | tf_op jit(solution)/shard_map/pallas_call | solution.py:173
  29.0 0.0 copy-start.5
  29.0 0.0 copy-start.2
  29.0 0.0 collective-permute-done.after_ref
  29.0 1.8 %shard_map.69.mine_ref.image_ref = bf16[3,64,1024]{2,1,0:T(8,128)(2,1)S(1)} custom-call(s32[16,1024]{1,0:T(8,128)S(1)} %copy-done.4, bf16[3,3,16,1024]{3,2,1,0:T(8,128)(2,1)S(1)} %bitcast.10, bf16[3,64,256]{2,1,0:T(8,128)(2,1)S(1)} %collective-permute-done.after_ref, bf16[3,64,1024]{2,1,0:T(8,128)(2,1)S(1)} %copy-done.1, ...), custom_call_target="tpu_custom_call" | custom-call | flops 2000000000 | bytes 1000000 | tf_op jit(solution)/shard_map/pallas_call | solution.py:173
  30.8 1.9 %collective-permute-start.2 = (bf16[3,64,1024]{2,1,0:T(8,128)(2,1)S(1)}, bf16[3,64,1024]{2,1,0:T(8,128)(2,1)S(1)}, u32[]{:S(2)}, u32[]{:S(2)}) collective-permute-start(bf16[3,64,1024]{2,1,0:T(8,128)(2,1)S(1)} %shard_map.69.mine_ref.image_ref), channel_id=1, source_target_pairs={{0,1},{1,0},{2,3},{3,2},{4,5},{5,4},{6,7},{7,6},{8,9},{9,8},{10,11... | collective-permute-start | bytes 1179656 | tf_op jit(solution)/shard_map/ppermute | solution.py:307
  32.8 0.0 copy-done.5
  32.8 0.0 copy-done.2
  32.8 0.9 %sampled.1.sampled_ref = f32[512,64]{1,0:T(8,128)S(1)} custom-call(s32[1,512]{1,0:T(1,128)S(1)} %bitcast.7, bf16[512,512]{1,0:T(8,128)(2,1)S(1)} %copy-done.2, bf16[3,64,1024]{2,1,0:T(8,128)(2,1)S(1)} %shard_map.69.mine_ref.image_ref), custom_call_target="tpu_custom_call" | custom-call | flops 2000000000 | bytes 2000000 | tf_op jit(solution)/shard_map/sampled/pallas_call | solution.py:205
  33.7 0.7 %collective-permute-done.2.theirs_ref = bf16[3,64,1024]{2,1,0:T(8,128)(2,1)S(1)} collective-permute-done((bf16[3,64,1024]{2,1,0:T(8,128)(2,1)S(1)}, bf16[3,64,1024]{2,1,0:T(8,128)(2,1)S(1)}, u32[]{:S(2)}, u32[]{:S(2)}) %collective-permute-start.2) | collective-permute-done | bytes 393248 | tf_op jit(solution)/shard_map/ppermute | solution.py:307
  34.4 0.0 all-to-all-done.basis_ref
  34.4 0.6 reduced.1
  35.0 1.9 %all-gather = f32[256,128]{1,0:T(8,128)S(1)} all-gather(f32[128,128]{1,0:T(8,128)S(1)} %get-tuple-element.11), channel_id=2, replica_groups=mesh['y'=4,'z'=16,'x'=4,'core'=2] {'core'}, dimensions={0}, use_global_device_ids=true | all-gather | bytes 196608 | tf_op jit(solution)/shard_map/all_gather | solution.py:311
  37.0 0.1 joined.1
  37.1 28.0 %all_to_all.10.pieces_ref = bf16[64,8,128]{2,1,0:T(8,128)(2,1)S(1)} all-to-all(bf16[64,8,128]{2,1,0:T(8,128)(2,1)S(1)} %bitcast.6), channel_id=1, replica_groups=mesh['y'=4,'z'=16,'x'=4,'core'=2] {'y','z'}, dimensions={0} | all-to-all | bytes 262144 | tf_op jit(solution)/shard_map/all_to_all | solution.py:313
  65.1 0.7 %totals.1 = (f32[8,64]{1,0:T(8,128)}, f32[8,64]{1,0:T(8,128)}) custom-call(bf16[64,8,128]{2,1,0:T(8,128)(2,1)S(1)} %all_to_all.10.pieces_ref), custom_call_target="tpu_custom_call" | custom-call | tf_op jit(solution)/shard_map/totals/pallas_call | solution.py:279
  (1 shorter events, 0.0 us)
Async XLA Ops:
  0.6 1.0 %copy-start = (bf16[3,64,1024]{2,1,0:T(8,128)(2,1)S(1)}, bf16[3,64,1024]{2,1,0:T(8,128)(2,1)}, u32[]{:S(2)}) copy-start(bf16[3,64,1024]{2,1,0:T(8,128)(2,1)} %basis_ref.7) | copy-start | bytes 1179652
  2.8 17.7 %copy-start.1 = (bf16[3,64,1024]{2,1,0:T(8,128)(2,1)S(1)}, bf16[3,64,1024]{2,1,0:T(8,128)(2,1)}, u32[]{:S(2)}) copy-start(bf16[3,64,1024]{2,1,0:T(8,128)(2,1)} %basis_ref.7) | copy-start | bytes 1179652
  2.9 17.7 %copy-start.3 = (bf16[16,3,3,1024]{3,0,2,1:T(8,128)(2,1)S(1)}, bf16[16,3,3,1024]{3,0,2,1:T(8,128)(2,1)}, u32[]{:S(2)}) copy-start(bf16[16,3,3,1024]{3,0,2,1:T(8,128)(2,1)} %param.6) | copy-start | bytes 884740
  2.9 17.7 %copy-start.4 = (s32[16,1024]{1,0:T(8,128)S(1)}, s32[16,1024]{1,0:T(8,128)}, u32[]{:S(2)}) copy-start(s32[16,1024]{1,0:T(8,128)} %columns_ref.5) | copy-start | bytes 196612
  2.9 31.6 %all-to-all-start = ((bf16[4,3,64,1024]{3,2,1,0:T(8,128)(2,1)}), bf16[4,3,64,1024]{3,2,1,0:T(8,128)(2,1)S(1)}, u32[]{:S(2)}, u32[]{:S(2)}) async-start(bf16[4,3,64,1024]{3,2,1,0:T(8,128)(2,1)} %get-tuple-element.7), calls=%async_computation | async-start | bytes 3145728 | tf_op jit(solution)/shard_map/all_to_all | solution.py:295
  7.3 21.7 %collective-permute-start = (bf16[3,64,256]{2,1,0:T(8,128)(2,1)S(1)}, bf16[3,64,256]{2,1,0:T(8,128)(2,1)S(1)}, u32[]{:S(2)}, u32[]{:S(2)}) collective-permute-start(bf16[3,64,256]{2,1,0:T(8,128)(2,1)S(1)} %get-tuple-element.8), channel_id=1, source_target_pairs={{8,0},{16,8},{24,16},{32,24},{40,32},{48,40},{56,48},{64,56},{72,6... | collective-permute-start | bytes 294920 | tf_op jit(solution)/shard_map/ppermute | solution.py:297
  18.6 8.6 %collective-permute-start.1 = (bf16[3,64,256]{2,1,0:T(8,128)(2,1)S(1)}, bf16[3,64,256]{2,1,0:T(8,128)(2,1)S(1)}, u32[]{:S(2)}, u32[]{:S(2)}) collective-permute-start(bf16[3,64,256]{2,1,0:T(8,128)(2,1)S(1)} %get-tuple-element.9), channel_id=1, source_target_pairs={{0,8},{8,16},{16,24},{24,32},{32,40},{40,48},{48,56},{56,64},{64,7... | collective-permute-start | bytes 294920 | tf_op jit(solution)/shard_map/ppermute | solution.py:296
  29.0 3.8 %copy-start.5 = (s32[512]{0:T(512)S(1)}, s32[512]{0:T(512)}, u32[]{:S(2)}) copy-start(s32[512]{0:T(512)} %param.8) | copy-start | bytes 6148
  29.0 3.8 %copy-start.2 = (bf16[512,512]{1,0:T(8,128)(2,1)S(1)}, bf16[512,512]{1,0:T(8,128)(2,1)}, u32[]{:S(2)}) copy-start(bf16[512,512]{1,0:T(8,128)(2,1)} %inverse_ref.1) | copy-start | bytes 1572868
  30.8 3.6 %collective-permute-start.2 = (bf16[3,64,1024]{2,1,0:T(8,128)(2,1)S(1)}, bf16[3,64,1024]{2,1,0:T(8,128)(2,1)S(1)}, u32[]{:S(2)}, u32[]{:S(2)}) collective-permute-start(bf16[3,64,1024]{2,1,0:T(8,128)(2,1)S(1)} %shard_map.69.mine_ref.image_ref), channel_id=1, source_target_pairs={{0,1},{1,0},{2,3},{3,2},{4,5},{5,4},{6,7},{7,6},{8,9},{9,8},{10,11... | collective-permute-start | bytes 1179656 | tf_op jit(solution)/shard_map/ppermute | solution.py:307
